TPU v7x, 256 devices: a whole 4x4x8 slice. The times are simulated.
256 devices in a mesh: dp: 8 (over x, core), ctx: 32 (over y, z).
Axes of the slice: x: 4, y: 4, z: 8, core: 2. Of those that a mesh axis runs over, the one named last changes fastest.
Arguments:
- features: bfloat16 [8, 4096, 6144], P('dp', 'ctx'), may hold values from -6 to 6
- upstream: bfloat16 [8, 4096, 2048], P('dp', 'ctx'), may hold values from -6 to 6
- lengths: int32 [8, 8], P('dp'), may hold values from 1 to 2048, 4096 in all within a row
- conv_taps: float32 [3, 6144], replicated, may hold values from -3 to 3
- residues: float32 [16, 2048], P(None, 'ctx'), may hold values from -0.12 to 0.12
- log_rate: float32 [16, 2048], P(None, 'ctx'), may hold values from -13.2 to -3.5
- skip_gain: float32 [2048], P('ctx'), may hold values from -4 to 4
Outputs:
- grad_features: bfloat16 [8, 4096, 6144], P('dp', 'ctx')
- grad_taps: float32 [3, 6144], replicated
- grad_residues: float32 [16, 2048], P(None, 'ctx')
- grad_skip: float32 [2048], P('ctx')
All inputs are finite; a program needn't handle non-finite values.
Results may differ from a plain program's by a relative error of at most 0.0095.
Values may be sent and summed in bfloat16 or wider, within the bound.
A program may use at most 192 MiB of HBM per device.

v0:
```python
import math

import jax
import jax.numpy as jnp
from jax import lax
from jax.sharding import PartitionSpec as P

BLOCK_ROWS = 128


def from_behind(block, axis, distance):
    devices = range(lax.axis_size(axis))
    route = [(i - distance, i) for i in devices if i - distance in devices]
    return lax.ppermute(block, axis, route)


def segment_of(positions, bounds):
    return jnp.sum((positions[:, None] >= bounds[None, :]).astype(jnp.int32), axis=1)


def segment_masks(positions, bounds, window_len):
    seg_ids = segment_of(positions, bounds)
    keep_one = ((positions >= 1) & (segment_of(positions - 1, bounds) == seg_ids)).astype(
        jnp.float32
    )
    keep_two = ((positions >= 2) & (segment_of(positions - 2, bounds) == seg_ids)).astype(
        jnp.float32
    )
    next_one = (
        (positions + 1 < window_len) & (segment_of(positions + 1, bounds) == seg_ids)
    ).astype(jnp.float32)
    next_two = (
        (positions + 2 < window_len) & (segment_of(positions + 2, bounds) == seg_ids)
    ).astype(jnp.float32)
    return (seg_ids, keep_one, keep_two, next_one, next_two)


def causal_taps(current, before, tap_rows, keep_one, keep_two):
    extended = jnp.concatenate([before, current], axis=0)
    return (
        tap_rows[0] * current
        + tap_rows[1] * (keep_one[:, None] * extended[1:-1])
        + tap_rows[2] * (keep_two[:, None] * extended[:-2])
    )


def transposed_taps(current, after, tap_rows, next_one, next_two):
    extended = jnp.concatenate([current, after], axis=0)
    return (
        tap_rows[0] * current
        + tap_rows[1] * (next_one[:, None] * extended[1:-1])
        + tap_rows[2] * (next_two[:, None] * extended[2:])
    )


def tap_terms(gradient, current, before, keep_one, keep_two):
    extended = jnp.concatenate([before, current], axis=0)
    first = jnp.sum(gradient * current, axis=0)
    second = jnp.sum(gradient * (keep_one[:, None] * extended[1:-1]), axis=0)
    third = jnp.sum(gradient * (keep_two[:, None] * extended[:-2]), axis=0)
    return jnp.stack([first, second, third])


def combine_states(earlier, later):
    return (earlier[0] * later[0], later[0] * earlier[1] + later[1])


def modal_sweep(source, segment_ids, decay_rate, coeff, other):
    length, chan_count = source.shape
    pole_count = decay_rate.shape[0]
    blocks = length // BLOCK_ROWS
    per_step = 4
    groups = blocks // per_step
    offsets = jnp.arange(BLOCK_ROWS, dtype=jnp.float32)
    rising = jnp.exp(decay_rate[None] * offsets[:, None, None])
    falling = jnp.exp(-decay_rate[None] * offsets[:, None, None])
    causal = offsets[:, None] >= offsets[None, :]

    def group_fn(inputs):
        src_blk, seg_blk, other_blk = inputs
        joined_mask = ((seg_blk[:, :, None] == seg_blk[:, None, :]) & causal[None]).astype(
            source.dtype
        )
        lifted = (src_blk[:, :, None, :] * rising[None]).reshape(
            per_step, BLOCK_ROWS, pole_count * chan_count
        )
        inner_state = jnp.einsum(
            "pij,pjk->pik", joined_mask, lifted, precision=lax.Precision.HIGHEST
        )
        inner_state = (
            inner_state.reshape(per_step, BLOCK_ROWS, pole_count, chan_count) * falling[None]
        )
        block_out = jnp.einsum("pimc,mc->pic", inner_state, coeff, precision=lax.Precision.HIGHEST)
        last_row = inner_state[:, -1]
        start_same = (seg_blk == seg_blk[:, :1]).astype(source.dtype)
        partial_sum = jnp.einsum(
            "pic,pimc->mc", other_blk, inner_state, precision=lax.Precision.HIGHEST
        )
        weights = jnp.einsum(
            "pic,imc->pmc",
            other_blk * start_same[:, :, None],
            falling,
            precision=lax.Precision.HIGHEST,
        )
        return (block_out, last_row, partial_sum, weights)

    src_groups = source.reshape(groups, per_step, BLOCK_ROWS, chan_count)
    seg_groups = segment_ids.reshape(groups, per_step, BLOCK_ROWS)
    other_groups = other.reshape(groups, per_step, BLOCK_ROWS, chan_count)
    block_out, last_row, partial_sum, weights = lax.map(
        group_fn, (src_groups, seg_groups, other_groups)
    )
    block_out = block_out.reshape(blocks, BLOCK_ROWS, chan_count)
    last_row = last_row.reshape(blocks, pole_count, chan_count)
    weights = weights.reshape(blocks, pole_count, chan_count)
    seg_rows = segment_ids.reshape(blocks, BLOCK_ROWS)
    starts = seg_rows[:, 0]
    finals = seg_rows[:, -1]
    joined = (starts[1:] == finals[:-1]).astype(source.dtype)
    through = (starts[:-1] == finals[:-1]).astype(source.dtype)
    one_step = jnp.exp(-decay_rate)
    block_decay = jnp.exp(-decay_rate * BLOCK_ROWS)
    factors = (joined * through)[:, None, None] * block_decay[None]
    inputs_in = joined[:, None, None] * one_step[None] * last_row[:-1]
    unused, states = lax.associative_scan(combine_states, (factors, inputs_in))
    carried = jnp.concatenate(
        [jnp.zeros((1, pole_count, chan_count), source.dtype), states], axis=0
    )
    start_rows = (seg_rows == starts[:, None]).astype(source.dtype)
    carry_out = (
        jnp.einsum("kmc,imc->kic", carried * coeff[None], falling, precision=lax.Precision.HIGHEST)
        * start_rows[:, :, None]
    )
    result = (block_out + carry_out).reshape(length, chan_count)
    grad_part = jnp.sum(partial_sum, axis=0) + jnp.einsum(
        "kmc,kmc->mc", weights, carried, precision=lax.Precision.HIGHEST
    )
    return (result, grad_part)


def per_device(features, upstream, lengths, conv_taps, residues, log_rate, skip_gain):
    feats = features[0]
    upf = upstream[0].astype(jnp.float32)
    tok_rows = feats.shape[0]
    channels = upstream.shape[2]
    ctx_count = lax.axis_size("ctx")
    shard_index = lax.axis_index("ctx")
    per_shard = channels // ctx_count
    window_len = tok_rows * ctx_count
    grad_scale = 1.0 / math.sqrt(window_len * lax.axis_size("dp"))
    bounds = jnp.cumsum(lengths[0])[:-1]
    local_pos = shard_index * tok_rows + jnp.arange(tok_rows, dtype=jnp.int32)
    seg_local, keep_one, keep_two, next_one, next_two = segment_masks(local_pos, bounds, window_len)
    whole_pos = jnp.arange(window_len, dtype=jnp.int32)
    seg_all, wkeep_one, wkeep_two, wnext_one, wnext_two = segment_masks(
        whole_pos, bounds, window_len
    )
    decay_rate = jnp.exp(log_rate)
    zero_rows = jnp.zeros((2, per_shard), jnp.float32)
    edge_rows = feats[-2:, :channels]
    before = from_behind(edge_rows, "ctx", 1).astype(jnp.float32)
    src_seq = feats[:, :channels].astype(jnp.float32)
    query_seq = causal_taps(src_seq, before, conv_taps[:, :channels], keep_one, keep_two)
    outgoing = feats[:, channels:].reshape(tok_rows, 2, channels)
    grad_out = (upf * query_seq).astype(jnp.bfloat16)[:, None, :]
    arrived = lax.all_to_all(outgoing, "ctx", split_axis=2, concat_axis=0, tiled=True)
    arrived_grad = lax.all_to_all(grad_out, "ctx", split_axis=2, concat_axis=0, tiled=True)
    tap_cols = lax.dynamic_slice(
        conv_taps.reshape(3, 3, channels), (0, 1, shard_index * per_shard), (3, 2, per_shard)
    )
    key_src = arrived[:, 0].astype(jnp.float32)
    val_src = arrived[:, 1].astype(jnp.float32)
    key_ch = causal_taps(key_src, zero_rows, tap_cols[:, 0], wkeep_one, wkeep_two)
    val_ch = causal_taps(val_src, zero_rows, tap_cols[:, 1], wkeep_one, wkeep_two)
    mixed_ch = (key_ch * val_ch).astype(jnp.bfloat16)
    mixedf = mixed_ch.astype(jnp.float32)
    conv_out, unused = modal_sweep(mixedf, seg_all, decay_rate, residues, jnp.zeros_like(mixedf))
    output_ch = (conv_out + skip_gain * mixedf).astype(jnp.bfloat16)
    gradf = arrived_grad[:, 0].astype(jnp.float32)
    adjoint, grad_resid = modal_sweep(
        gradf[::-1], seg_all[::-1], decay_rate, residues, mixedf[::-1]
    )
    grad_mixed = (adjoint[::-1] + skip_gain * gradf).astype(jnp.bfloat16)
    skip_part = jnp.sum(mixedf * gradf, axis=0)
    dmixf = grad_mixed.astype(jnp.float32)
    grad_key = dmixf * val_ch
    grad_val = dmixf * key_ch
    key_back = transposed_taps(grad_key, zero_rows, tap_cols[:, 0], wnext_one, wnext_two)
    val_back = transposed_taps(grad_val, zero_rows, tap_cols[:, 1], wnext_one, wnext_two)
    second = jnp.stack([key_back, val_back], axis=1).astype(jnp.bfloat16)
    kv_taps = jnp.stack(
        [
            tap_terms(grad_key, key_src, zero_rows, wkeep_one, wkeep_two),
            tap_terms(grad_val, val_src, zero_rows, wkeep_one, wkeep_two),
        ],
        axis=1,
    )
    first = output_ch[:, None, :]
    first_back = lax.all_to_all(first, "ctx", split_axis=0, concat_axis=2, tiled=True)
    second_back = lax.all_to_all(second, "ctx", split_axis=0, concat_axis=2, tiled=True)
    grad_query = upf * first_back[:, 0].astype(jnp.float32)
    rows_next = from_behind(grad_query[:2], "ctx", -1)
    grad_query_feats = transposed_taps(
        grad_query, rows_next, conv_taps[:, :channels], next_one, next_two
    ).astype(jnp.bfloat16)
    grad_feats = jnp.concatenate(
        [grad_query_feats, second_back.reshape(tok_rows, 2 * channels)], axis=1
    )
    placed = (
        jnp.zeros((3, 3, channels), jnp.float32)
        .at[:, 0, :]
        .set(tap_terms(grad_query, src_seq, before, keep_one, keep_two))
    )
    placed = lax.dynamic_update_slice(placed, kv_taps, (0, 1, shard_index * per_shard))
    tap_sum = placed.reshape(3, 3 * channels)
    grad_taps = lax.psum(tap_sum, ("dp", "ctx")) * grad_scale
    resid_sum, skip_sum = lax.psum((grad_resid, skip_part), "dp")
    return (grad_feats[None], grad_taps, resid_sum * grad_scale, skip_sum * grad_scale)


def solution(mesh):
    return jax.shard_map(
        per_device,
        mesh=mesh,
        in_specs=(
            P("dp", "ctx", None),
            P("dp", "ctx", None),
            P("dp", None),
            P(),
            P(None, "ctx"),
            P(None, "ctx"),
            P("ctx"),
        ),
        out_specs=(P("dp", "ctx", None), P(), P(None, "ctx"), P("ctx")),
        check_vma=False,
    )
```

profile of v0, /device:TPU:1, one launch (start us, length us, event | category | flops | bytes accessed | tf_op | source)
XLA Modules:
  0.0 609.8 jit_solution(1691059669882293001)
XLA Ops:
  10.4 5.2 collective-permute-start.1
  17.9 7.7 %collective-permute-done.1 = bf16[2,2048]{0,1:T(8,128)(2,1)} collective-permute-done((bf16[2,2048]{0,1:T(8,128)(2,1)}, bf16[2,2048]{0,1:T(8,128)(2,1)}, u32[]{:S(2)}, u32[]{:S(2)}) %collective-permute-start.1) | collective-permute-done | bytes 8224 | tf_op jit(solution)/shard_map/ppermute | solution.py:14
  28.8 8.9 %copy.348 = bf16[128,1,2048]{0,1,2:T(2,128)(2,1)} copy(bf16[128,1,2048]{0,2,1:T(8,128)(2,1)S(1)} %fusion.46) | data formatting | bytes 1048576 | tf_op jit(solution)/shard_map/broadcast_in_dim | solution.py:165
  38.2 12.5 %reduce.26 = bf16[2048,128]{1,0:T(8,128)(2,1)S(1)} reduce(bf16[2048,1,128]{2,1,0:T(2,128)(2,1)} %bitcast.298, bf16[]{:T(256)} %broadcast.332), dimensions={1}, to_apply=%bitcast.221.reduce_sub_computation | reduce | bytes 1048578
  51.7 13.2 %all-to-all-start.2 = ((bf16[32,2,4096]{2,1,0:T(2,128)(2,1)}), bf16[32,2,4096]{2,1,0:T(2,128)(2,1)S(1)}, u32[]{:S(2)}, u32[]{:S(2)}) async-start(bf16[32,2,4096]{2,1,0:T(2,128)(2,1)} %reshape.467), calls=%async_computation.2 | async-start | bytes 1048576 | tf_op jit(solution)/shard_map/all_to_all | solution.py:167
  65.0 9.5 %copy.215 = bf16[128,2,2048]{0,1,2:T(2,128)(2,1)} copy(bf16[128,2,2048]{0,2,1:T(8,128)(2,1)S(1)} %bitcast.297) | data formatting | bytes 2097152 | tf_op jit(solution)/shard_map/reshape | solution.py:164
  77.7 8.6 %all-to-all-start = ((bf16[128,2,2048]{0,1,2:T(2,128)(2,1)}), bf16[128,2,2048]{0,1,2:T(2,128)(2,1)S(1)}, u32[]{:S(2)}, u32[]{:S(2)}) async-start(bf16[128,2,2048]{0,1,2:T(2,128)(2,1)} %copy.215), calls=%async_computation | async-start | bytes 2097152 | tf_op jit(solution)/shard_map/all_to_all | solution.py:166
  92.9 13.4 %rev.13 = f32[4096,64]{0,1:T(8,128)S(1)} reverse(f32[4096,64]{0,1:T(8,128)} %bitcast.302), dimensions={0} | reverse | bytes 2097152 | tf_op jit(solution)/shard_map/rev | solution.py:181
  112.3 3.6 multiply_reduce_fusion.2
  122.3 90.9 %while.32 = (s32[]{:T(128)}, f32[8,4,128,64]{2,1,0,3:T(4,128)S(1)}, f32[8,4,16,64]{3,2,1,0:T(8,128)S(1)}, f32[8,16,64]{2,1,0:T(8,128)}, f32[8,4,16,64]{3,2,1,0:T...) while((s32[]{:T(128)}, f32[8,4,128,64]{2,1,0,3:T(4,128)S(1)}, ...), condition=%wide.region_12.13_spmd.clone, body=%wide.region_11.12_spmd.clone.sunk | while | flops 820528128 | bytes 18125500 | solution.py:110
  129.3 3.5 fusion.87
  140.6 3.5 fusion.87
  152.0 3.5 fusion.87
  163.3 3.5 fusion.87
  174.6 3.5 fusion.87
  186.0 3.5 fusion.87
  215.4 52.8 %while.31 = (s32[]{:T(128)}, f32[8,4,128,64]{2,1,0,3:T(4,128)}, f32[8,4,16,64]{3,2,1,0:T(8,128)}, s32[8,4,128]{2,1,0:T(4,128)S(1)}, f32[8,4,128,64]{2,1,0,3:T(4,...) while((s32[]{:T(128)}, f32[8,4,128,64]{2,1,0,3:T(4,128)}, ...), condition=%wide.region_5.6_spmd.clone, body=%wide.region_4.5_spmd.clone.sunk | while | flops 807780352 | bytes 14388493 | solution.py:110
  294.5 8.6 %all-to-all-start.1 = ((bf16[32,2,4096]{2,1,0:T(2,128)(2,1)}), bf16[32,2,4096]{2,1,0:T(2,128)(2,1)}, u32[]{:S(2)}, u32[]{:S(2)}) async-start(bf16[32,2,4096]{2,1,0:T(2,128)(2,1)} %reshape.471), calls=%async_computation.1 | async-start | bytes 1048576 | tf_op jit(solution)/shard_map/all_to_all | solution.py:199
  309.8 14.4 %all-reduce.23 = (f32[16,64]{1,0:T(8,128)S(1)}, f32[64]{0:T(128)S(1)}) all-reduce(f32[16,64]{1,0:T(8,128)S(1)} %add.336, f32[64]{0:T(128)S(1)} %copy-done.70), channel_id=1, replica_groups=mesh['dp'=8,'ctx'=32] {'dp'}, use_global_device_ids=true, to_apply=%region_26.27 | all-reduce | flops 1088 | bytes 8704 | tf_op jit(solution)/shard_map/psum | solution.py:217
  325.3 9.2 %all-to-all-start.3 = ((bf16[32,2,8192]{2,1,0:T(2,128)(2,1)}), bf16[32,2,8192]{2,1,0:T(2,128)(2,1)S(1)}, u32[]{:S(2)}, u32[]{:S(2)}) async-start(bf16[32,2,8192]{2,1,0:T(2,128)(2,1)} %reshape.469), calls=%async_computation.3 | async-start | bytes 2097152 | tf_op jit(solution)/shard_map/all_to_all | solution.py:200
  334.6 4.1 reshape.472
  338.8 3.6 copy.226
  351.0 6.3 %collective-permute-done = f32[2,2048]{1,0:T(2,128)S(1)} collective-permute-done((f32[2,2048]{1,0:T(2,128)S(1)}, f32[2,2048]{1,0:T(2,128)S(1)}, u32[]{:S(2)}, u32[]{:S(2)}) %collective-permute-start) | collective-permute-done | bytes 16416 | tf_op jit(solution)/shard_map/ppermute | solution.py:14
  360.5 233.8 %all-reduce.26.cloned.1.call-done = f32[3,6144]{1,0:T(4,128)} async-done(((f32[3,6144]{1,0:T(4,128)}), f32[3,6144]{1,0:T(4,128)}) %all-reduce.26.cloned.1.call-update) | async-done | bytes 73744 | tf_op jit(solution)/shard_map/psum | solution.py:216
  (665 shorter events, 208.3 us)
Async XLA Ops:
  9.1 55.8 %copy-start.2 = (bf16[1,128,6144]{1,2,0:T(8,128)(2,1)}, bf16[1,128,6144]{1,2,0:T(8,128)(2,1)S(1)}, u32[]{:S(2)}) copy-start(bf16[1,128,6144]{1,2,0:T(8,128)(2,1)S(1)} %copy.214) | copy-start | bytes 4718596
  10.4 15.3 %collective-permute-start.1 = (bf16[2,2048]{0,1:T(8,128)(2,1)}, bf16[2,2048]{0,1:T(8,128)(2,1)}, u32[]{:S(2)}, u32[]{:S(2)}) collective-permute-start(bf16[2,2048]{0,1:T(8,128)(2,1)} %slice.487), channel_id=1, source_target_pairs={{0,1},{1,2},{2,3},{3,4},{4,5},{5,6},{6,7},{7,8},{8,9},{9,10},{10,1... | collective-permute-start | bytes 24584 | tf_op jit(solution)/shard_map/ppermute | solution.py:14
  15.6 13.1 %copy-start.9 = (f32[128,2048]{0,1:T(8,128)}, f32[128,2048]{0,1:T(8,128)S(1)}, u32[]{:S(2)}) copy-start(f32[128,2048]{0,1:T(8,128)S(1)} %slice_convert_fusion) | copy-start | bytes 3145732
  15.9 12.8 %copy-start.38 = (f32[1,2048]{1,0:T(1,128)}, f32[1,2048]{1,0:T(1,128)S(1)}, u32[]{:S(2)}) copy-start(f32[1,2048]{1,0:T(1,128)S(1)} %get-tuple-element.452) | copy-start | bytes 24580
  15.9 12.8 %copy-start.40 = (f32[1,2048]{1,0:T(1,128)}, f32[1,2048]{1,0:T(1,128)S(1)}, u32[]{:S(2)}) copy-start(f32[1,2048]{1,0:T(1,128)S(1)} %get-tuple-element.453) | copy-start | bytes 24580
  15.9 12.8 %copy-start.42 = (f32[1,2048]{1,0:T(1,128)}, f32[1,2048]{1,0:T(1,128)S(1)}, u32[]{:S(2)}) copy-start(f32[1,2048]{1,0:T(1,128)S(1)} %get-tuple-element.454) | copy-start | bytes 24580
  16.6 12.1 %copy-start.50 = (f32[128]{0:T(128)}, f32[128]{0:T(128)S(1)}, u32[]{:S(2)}) copy-start(f32[128]{0:T(128)S(1)} %get-tuple-element.477) | copy-start | bytes 1540
  16.6 12.1 %copy-start.52 = (f32[128]{0:T(128)}, f32[128]{0:T(128)S(1)}, u32[]{:S(2)}) copy-start(f32[128]{0:T(128)S(1)} %get-tuple-element.478) | copy-start | bytes 1540
  51.7 26.0 %all-to-all-start.2 = ((bf16[32,2,4096]{2,1,0:T(2,128)(2,1)}), bf16[32,2,4096]{2,1,0:T(2,128)(2,1)S(1)}, u32[]{:S(2)}, u32[]{:S(2)}) async-start(bf16[32,2,4096]{2,1,0:T(2,128)(2,1)} %reshape.467), calls=%async_computation.2 | async-start | bytes 1048576 | tf_op jit(solution)/shard_map/all_to_all | solution.py:167
  77.7 33.2 %all-to-all-start = ((bf16[128,2,2048]{0,1,2:T(2,128)(2,1)}), bf16[128,2,2048]{0,1,2:T(2,128)(2,1)S(1)}, u32[]{:S(2)}, u32[]{:S(2)}) async-start(bf16[128,2,2048]{0,1,2:T(2,128)(2,1)} %copy.215), calls=%async_computation | async-start | bytes 2097152 | tf_op jit(solution)/shard_map/all_to_all | solution.py:166
  86.4 25.9 %copy-start.54 = (f32[64]{0:T(128)}, f32[64]{0:T(128)S(1)}, u32[]{:S(2)}) copy-start(f32[64]{0:T(128)S(1)} %get-tuple-element.446) | copy-start | bytes 772
  86.4 25.9 %copy-start.56 = (f32[64]{0:T(128)}, f32[64]{0:T(128)S(1)}, u32[]{:S(2)}) copy-start(f32[64]{0:T(128)S(1)} %get-tuple-element.447) | copy-start | bytes 772
  86.4 25.9 %copy-start.58 = (f32[64]{0:T(128)}, f32[64]{0:T(128)S(1)}, u32[]{:S(2)}) copy-start(f32[64]{0:T(128)S(1)} %get-tuple-element.448) | copy-start | bytes 772
  86.4 25.9 %copy-start.60 = (f32[64]{0:T(128)}, f32[64]{0:T(128)S(1)}, u32[]{:S(2)}) copy-start(f32[64]{0:T(128)S(1)} %get-tuple-element.449) | copy-start | bytes 772
  86.4 25.8 %copy-start.62 = (f32[64]{0:T(128)}, f32[64]{0:T(128)S(1)}, u32[]{:S(2)}) copy-start(f32[64]{0:T(128)S(1)} %get-tuple-element.450) | copy-start | bytes 772
  86.4 25.8 %copy-start.64 = (f32[64]{0:T(128)}, f32[64]{0:T(128)S(1)}, u32[]{:S(2)}) copy-start(f32[64]{0:T(128)S(1)} %get-tuple-element.451) | copy-start | bytes 772
  89.0 23.3 %copy-start.34 = (f32[4096]{0:T(1024)}, f32[4096]{0:T(1024)S(1)}, u32[]{:S(2)}) copy-start(f32[4096]{0:T(1024)S(1)} %get-tuple-element.468) | copy-start | bytes 49156
  89.0 23.3 %copy-start.36 = (f32[4096]{0:T(1024)}, f32[4096]{0:T(1024)S(1)}, u32[]{:S(2)}) copy-start(f32[4096]{0:T(1024)S(1)} %get-tuple-element.469) | copy-start | bytes 49156
  291.4 11.7 %copy-start.61 = (f32[64]{0:T(128)S(1)}, f32[64]{0:T(128)}, u32[]{:S(2)}) copy-start(f32[64]{0:T(128)} %copy-done.60) | copy-start | bytes 772
  291.4 11.7 %copy-start.63 = (f32[64]{0:T(128)S(1)}, f32[64]{0:T(128)}, u32[]{:S(2)}) copy-start(f32[64]{0:T(128)} %copy-done.62) | copy-start | bytes 772
  294.5 30.8 %all-to-all-start.1 = ((bf16[32,2,4096]{2,1,0:T(2,128)(2,1)}), bf16[32,2,4096]{2,1,0:T(2,128)(2,1)}, u32[]{:S(2)}, u32[]{:S(2)}) async-start(bf16[32,2,4096]{2,1,0:T(2,128)(2,1)} %reshape.471), calls=%async_computation.1 | async-start | bytes 1048576 | tf_op jit(solution)/shard_map/all_to_all | solution.py:199
  325.3 270.5 %all-to-all-start.3 = ((bf16[32,2,8192]{2,1,0:T(2,128)(2,1)}), bf16[32,2,8192]{2,1,0:T(2,128)(2,1)S(1)}, u32[]{:S(2)}, u32[]{:S(2)}) async-start(bf16[32,2,8192]{2,1,0:T(2,128)(2,1)} %reshape.469), calls=%async_computation.3 | async-start | bytes 2097152 | tf_op jit(solution)/shard_map/all_to_all | solution.py:200
  334.6 259.7 %all-reduce.26.cloned.1.call-start = ((), (), s32[]{:S(2)}) async-start(), calls=%async_computation.4 | async-start | bytes 196608 | tf_op jit(solution)/shard_map/psum | solution.py:216
  348.5 8.8 %collective-permute-start = (f32[2,2048]{1,0:T(2,128)S(1)}, f32[2,2048]{1,0:T(2,128)S(1)}, u32[]{:S(2)}, u32[]{:S(2)}) collective-permute-start(f32[2,2048]{1,0:T(2,128)S(1)} %copy.228), channel_id=1, source_target_pairs={{1,0},{2,1},{3,2},{4,3},{5,4},{6,5},{7,6},{8,7},{9,8},{10,9},{11,1... | collective-permute-start | bytes 49160 | tf_op jit(solution)/shard_map/ppermute | solution.py:14
  (98 other events, 338.2 us)
Sparse Core Ops, SparseCore 0:
  351.1 243.1 all-reduce.25
where the time goes:
time: 621 us; the launch traced here: 610 us
  waiting for transfers between devices  252 us (41%)
  local copies, waits for them, and re-layouts  151 us (24%)
  other arithmetic  67.8 us (11%)
  matrix products  60.7 us (10%)
  starting transfers between devices  46 us (7%)
  between operations  15.7 us (3%)
  blocking collectives  14.4 us (2%)
    psum x1, waiting for transfers between devices, per_device(): grad_taps = lax.psum(tap_sum, ('dp', 'ctx')) * grad_scale  234 us
    dot_general x8, matrix products, group_fn(): jnp.einsum('pic,pimc->mc', other_blk, inner_state, precision=lax.Precisio...  27.9 us
    unnamed x151, local copies, waits for them, and re-layouts  23.1 us
    dynamic_slice x40, local copies, waits for them, and re-layouts, modal_sweep(): lax.map(group_fn, (src_groups, seg_groups, other_groups))  22.3 us
    dot_general x16, matrix products, group_fn(): jnp.einsum('pij,pjk->pik', joined_mask, lifted, precision=lax.Precision.H...  19.2 us
    slice x16, local copies, waits for them, and re-layouts, group_fn(): last_row = inner_state[:, -1]  18.7 us
    dynamic_update_slice x64, local copies, waits for them, and re-layouts, modal_sweep(): lax.map(group_fn, (src_groups, seg_groups, other_groups))  18.4 us
    psum x1, blocking collectives, per_device(): resid_sum, skip_sum = lax.psum((grad_resid, skip_part), 'dp')  14.4 us
  transfers between devices with their start and end apart: 7, of which 5 were waited for; matrix products, arithmetic and copies ran while one was open for 10% of the time, Pallas kernels for 0%

commit v1 on v0

v1 whole, which is shorter than its diff:
```python
import functools
import math

import jax
import jax.numpy as jnp
from jax import lax
from jax.experimental import pallas as pl
from jax.experimental.pallas import tpu as pltpu
from jax.sharding import PartitionSpec as P

MESH = pl.DeviceIdType.MESH
F32 = jnp.float32
BF16 = jnp.bfloat16
LANES = 128
SUBS = 8
GROUP = 4


def row_iota(rows):
    return lax.broadcasted_iota(jnp.int32, (rows, LANES), 0)


def lane_low(rows):
    return lax.broadcasted_iota(jnp.int32, (rows, LANES), 1) < LANES // 2


def swap_halves(x):
    return pltpu.roll(x, LANES // 2, 1)


def join_pair(low, high, first):
    mask = lane_low(low.shape[0])
    if first:
        return jnp.where(mask, low, swap_halves(high))
    return jnp.where(mask, swap_halves(low), high)


def split_pair(a, b):
    mask = lane_low(a.shape[0])
    return jnp.where(mask, a, swap_halves(b)), jnp.where(mask, swap_halves(a), b)


def free_of(bounds, low, high):
    clear = None
    for bound in bounds:
        one = (low > bound) | (high < bound)
        clear = one if clear is None else clear & one
    return jnp.where(clear, 1.0, 0.0).astype(F32)


def kernel(
    ctx,
    dp,
    scale,
    lengths,
    feats,
    upstream,
    taps,
    own,
    own_skip,
    grad_feats,
    grad_taps,
    grad_res,
    grad_skip,
    params,
    skips,
    halo,
    first_out,
    first_in,
    carry_out,
    carry_in,
    prefixes,
    joins,
    source,
    gradient,
    output,
    adjoint,
    decay,
    coeff,
    gain,
    state,
    costate,
    res_sum,
    skip_sum,
    masks,
    edge_out,
    edge_in,
    tail,
    tap_part,
    part_out,
    part_in,
    dp_out,
    dp_in,
    tap_out,
    tap_in,
    send_sem,
    recv_sem,
):
    rows, channels = upstream.shape
    poles = own.shape[0]
    groups = channels // LANES
    halves = groups // SUBS
    half_rows = rows * SUBS
    pole_rows = poles * SUBS
    steps = rows // SUBS
    window = rows * ctx
    me = lax.axis_index("ctx")
    my_dp = lax.axis_index("dp")

    def peer_of(o):
        return lax.rem(me + o, ctx)

    barrier = pltpu.get_barrier_semaphore()

    def greet(o, c):
        pl.semaphore_signal(barrier, inc=1, device_id={"ctx": peer_of(o)}, device_id_type=MESH)
        return c

    lax.fori_loop(1, ctx, greet, 0)

    def greet_dp(o, c):
        pl.semaphore_signal(barrier, inc=1, device_id={"dp": lax.rem(my_dp + o, dp)}, device_id_type=MESH)
        return c

    lax.fori_loop(1, dp, greet_dp, 0)
    pl.semaphore_wait(barrier, ctx - 1 + dp - 1)

    def remote(src, dst, k, to):
        return pltpu.make_async_remote_copy(
            src_ref=src, dst_ref=dst, send_sem=send_sem.at[k], recv_sem=recv_sem.at[k], device_id=to, device_id_type=MESH
        )

    halo_copy = remote(feats.at[pl.ds(rows - SUBS, SUBS)], halo, 0, {"ctx": peer_of(1)})
    halo_copy.start()

    def send_params(o, c):
        to = {"ctx": peer_of(o)}
        remote(own, params.at[me], 1, to).start()
        remote(own_skip, skips.at[me], 2, to).start()
        return c

    lax.fori_loop(1, ctx, send_params, 0)
    params[pl.ds(me, 1)] = own[...][None]
    skips[pl.ds(me, 1)] = own_skip[...][None]

    bounds = [0]
    total = 0
    for j in range(lengths.shape[1] - 1):
        total = total + lengths[0, j]
        bounds.append(total)
    bounds.append(window)
    start = me * rows
    pos = start + row_iota(rows)
    keep_one = free_of(bounds, pos, pos)
    keep_two = free_of(bounds, pos - 1, pos)
    next_one = free_of(bounds, pos + 1, pos + 1)
    next_two = free_of(bounds, pos + 1, pos + 2)
    masks[0] = keep_one
    masks[1] = keep_two
    masks[2] = next_one
    masks[3] = next_two
    masks[4] = free_of(bounds, pos + 1, start + rows - 1 + 0 * pos)
    masks[5] = free_of(bounds, start + 1 + 0 * pos, pos)
    row = row_iota(rows)
    masks[6] = jnp.where(row < rows - 1, next_one, 0.0)
    masks[7] = jnp.where(row < rows - 2, next_two, 0.0)

    low16 = lane_low(poles)

    def join_masks(k, c):
        low = jnp.where(low16, k * rows, (ctx - 1 - k) * rows + 1)
        joins[k] = free_of(bounds, low, low + (rows - 1))
        return c

    lax.fori_loop(0, ctx, join_masks, 0)

    halo_copy.wait()

    def shifted(off):
        f = feats[:, pl.ds(off, LANES)].astype(F32)
        ext = jnp.concatenate([halo[:, pl.ds(off, LANES)].astype(F32), f], axis=0)
        one = masks[0] * pltpu.roll(ext, 1, 0)[SUBS:]
        two = masks[1] * pltpu.roll(ext, 2, 0)[SUBS:]
        return f, one, two

    def featured(off, parts):
        lanes = pl.ds(off, LANES)
        return taps[0:1, lanes] * parts[0] + taps[1:2, lanes] * parts[1] + taps[2:3, lanes] * parts[2]

    def at(i, third):
        return pl.multiple_of(third * channels + i * LANES, LANES)

    def strided(i, count, stride_rows):
        return pl.ds(lax.div(i, SUBS) * stride_rows + lax.rem(i, SUBS), count, stride=SUBS)

    def enter(i, c):
        query = featured(at(i, 0), shifted(at(i, 0)))
        key = featured(at(i, 1), shifted(at(i, 1)))
        value = featured(at(i, 2), shifted(at(i, 2)))
        up = upstream[:, pl.ds(at(i, 0), LANES)].astype(F32)
        source[strided(i, rows, half_rows), :] = (key * value).astype(BF16).astype(F32)
        gradient[strided(i, rows, half_rows), :] = (up * query).astype(BF16).astype(F32)
        return c

    lax.fori_loop(0, groups, enter, 0)

    def wait_all(buf, k, slots):
        pltpu.make_async_copy(buf.at[pl.ds(0, slots)], buf.at[pl.ds(0, slots)], recv_sem.at[k]).wait()

    def wait_sent(buf, k, slots):
        pltpu.make_async_copy(buf.at[pl.ds(0, slots)], buf.at[pl.ds(0, slots)], send_sem.at[k]).wait()

    wait_all(params, 1, ctx - 1)
    wait_all(skips, 2, ctx - 1)

    def spread(i, c):
        low, high = params[2 * i], params[2 * i + 1]
        coeff[strided(i, poles, pole_rows), :] = join_pair(low, high, True)
        decay[strided(i, poles, pole_rows), :] = jnp.exp(-jnp.exp(join_pair(low, high, False)))
        low_s = jnp.broadcast_to(skips[2 * i], (SUBS, LANES))
        high_s = jnp.broadcast_to(skips[2 * i + 1], (SUBS, LANES))
        gain[pl.ds(i, 1), :] = join_pair(low_s, high_s, True)[0:1]
        return c

    lax.fori_loop(0, groups, spread, 0)

    def half_ends(h, c):
        pole_at = pl.ds(pl.multiple_of(h * pole_rows, SUBS), pole_rows)
        fac = decay[pole_at, :].reshape(poles, SUBS, LANES)

        def chunk(k, carry):
            s, u = carry
            back = steps - 1 - k
            x = source[pl.ds(pl.multiple_of(h * half_rows + k * 64, 64), 64), :].reshape(SUBS, SUBS, LANES)
            g = gradient[pl.ds(pl.multiple_of(h * half_rows + back * 64, 64), 64), :].reshape(SUBS, SUBS, LANES)
            mx = masks[4, pl.ds(pl.multiple_of(k * SUBS, SUBS), SUBS), :]
            mg = masks[5, pl.ds(pl.multiple_of(back * SUBS, SUBS), SUBS), :]
            for t in range(SUBS):
                r = SUBS - 1 - t
                s = s * fac + (x[t] * mx[t : t + 1])[None]
                u = u * fac + (g[r] * mg[r : r + 1])[None]
            return s, u

        zero = jnp.zeros((poles, SUBS, LANES), F32)
        s, u = lax.fori_loop(0, steps, chunk, (zero, zero))
        state[pole_at, :] = s.reshape(pole_rows, LANES)
        costate[pole_at, :] = u.reshape(pole_rows, LANES)
        return c

    lax.fori_loop(0, halves, half_ends, 0)

    def pack_first(i, c):
        a = state[strided(i, poles, pole_rows), :]
        b = costate[strided(i, poles, pole_rows), :]
        low, high = split_pair(a, b)
        first_out[2 * i] = low.astype(BF16)
        first_out[2 * i + 1] = high.astype(BF16)
        return c

    lax.fori_loop(0, groups, pack_first, 0)

    def exchange(out, into, k):
        def send(o, c):
            to = peer_of(o)
            remote(out.at[to], into.at[me], k, {"ctx": to}).start()
            return c

        lax.fori_loop(1, ctx, send, 0)
        into[pl.ds(me, 1)] = out[pl.ds(me, 1)]

    exchange(first_out, first_in, 3)
    wait_all(first_in, 3, ctx - 1)

    own_rate = jnp.where(low16, swap_halves(own[...]), own[...])
    block_decay = jnp.exp(-jnp.exp(own_rate) * rows)

    def scan(k, w):
        prefixes[k] = w
        here = jnp.where(low16, first_in[k].astype(F32), first_in[ctx - 1 - k].astype(F32))
        return joins[k] * block_decay * w + here

    lax.fori_loop(0, ctx, scan, jnp.zeros((poles, LANES), F32))

    def pack_carry(k, c):
        carry_out[k] = jnp.where(low16, prefixes[k], prefixes[ctx - 1 - k]).astype(BF16)
        return c

    lax.fori_loop(0, ctx, pack_carry, 0)
    exchange(carry_out, carry_in, 4)
    wait_all(carry_in, 4, ctx - 1)

    def unpack_carry(i, c):
        low, high = carry_in[2 * i].astype(F32), carry_in[2 * i + 1].astype(F32)
        state[strided(i, poles, pole_rows), :] = join_pair(low, high, True)
        costate[strided(i, poles, pole_rows), :] = join_pair(low, high, False)
        return c

    lax.fori_loop(0, groups, unpack_carry, 0)

    res_sum[...] = jnp.zeros_like(res_sum)
    skip_sum[...] = jnp.zeros_like(skip_sum)

    def half_sweep(h, c):
        skip = gain[pl.ds(pl.multiple_of(h * SUBS, SUBS), SUBS), :]

        def chunk(k, c):
            back = steps - 1 - k
            at_x = pl.ds(pl.multiple_of(h * half_rows + k * 64, 64), 64)
            at_g = pl.ds(pl.multiple_of(h * half_rows + back * 64, 64), 64)
            x = source[at_x, :].reshape(SUBS, SUBS, LANES)
            gx = gradient[at_x, :].reshape(SUBS, SUBS, LANES)
            g = gradient[at_g, :].reshape(SUBS, SUBS, LANES)
            keep = masks[0, pl.ds(pl.multiple_of(k * SUBS, SUBS), SUBS), :]
            keep_g = masks[2, pl.ds(pl.multiple_of(back * SUBS, SUBS), SUBS), :]
            out = [skip * x[t] for t in range(SUBS)]
            adj = [skip * g[t] for t in range(SUBS)]
            for p in range(0, poles, GROUP):
                here = pl.ds(pl.multiple_of(h * pole_rows + p * SUBS, SUBS), GROUP * SUBS)
                shape = (GROUP, SUBS, LANES)
                s = state[here, :].reshape(shape)
                u = costate[here, :].reshape(shape)
                fac = decay[here, :].reshape(shape)
                res = coeff[here, :].reshape(shape)
                acc = res_sum[here, :].reshape(shape)
                for t in range(SUBS):
                    r = SUBS - 1 - t
                    s = s * (fac * keep[t : t + 1][None]) + x[t][None]
                    out[t] = out[t] + jnp.sum(res * s, axis=0)
                    acc = acc + s * gx[t][None]
                    u = u * (fac * keep_g[r : r + 1][None]) + g[r][None]
                    adj[r] = adj[r] + jnp.sum(res * u, axis=0)
                state[here, :] = s.reshape(GROUP * SUBS, LANES)
                costate[here, :] = u.reshape(GROUP * SUBS, LANES)
                res_sum[here, :] = acc.reshape(GROUP * SUBS, LANES)
            output[at_x, :] = jnp.stack(out).reshape(SUBS * SUBS, LANES)
            adjoint[at_g, :] = jnp.stack(adj).reshape(SUBS * SUBS, LANES)
            both = pl.ds(pl.multiple_of(h * SUBS, SUBS), SUBS)
            skip_sum[both, :] = skip_sum[both, :] + jnp.sum(x * gx, axis=0)
            return c

        lax.fori_loop(0, steps, chunk, 0)
        return c

    lax.fori_loop(0, halves, half_sweep, 0)

    tap_part[...] = jnp.zeros_like(tap_part)

    def leave(i, c):
        out = output[strided(i, rows, half_rows), :].astype(BF16).astype(F32)
        mixed = adjoint[strided(i, rows, half_rows), :].astype(BF16).astype(F32)
        up = upstream[:, pl.ds(at(i, 0), LANES)].astype(F32)
        parts = [shifted(at(i, third)) for third in range(3)]
        key = featured(at(i, 1), parts[1])
        value = featured(at(i, 2), parts[2])
        here = pl.ds(at(i, 0), LANES)
        for third, post in enumerate((up * out, mixed * value, mixed * key)):
            lanes = pl.ds(at(i, third), LANES)
            for j in range(3):
                tap_part[third * 3 + j : third * 3 + j + 1, here] = jnp.sum(post * parts[third][j], axis=0, keepdims=True)
            edge_out[:, lanes] = post[0:2]
            back = (
                taps[0:1, lanes] * post
                + taps[1:2, lanes] * (masks[6] * pltpu.roll(post, rows - 1, 0))
                + taps[2:3, lanes] * (masks[7] * pltpu.roll(post, rows - 2, 0))
            )
            grad_feats[:, lanes] = back.astype(BF16)
            tail[:, lanes] = back[rows - 16 :]
        tap_part[9:10, here] = skip_sum[pl.ds(i, 1), :]
        return c

    lax.fori_loop(0, groups, leave, 0)
    edge_copy = remote(edge_out, edge_in, 5, {"ctx": peer_of(ctx - 1)})
    edge_copy.start()

    def pack_parts(i, c):
        a = res_sum[strided(i, poles, pole_rows), :]
        b = tap_part[:, pl.ds(at(i, 0), LANES)]
        low, high = split_pair(a, b)
        part_out[2 * i] = low
        part_out[2 * i + 1] = high
        return c

    lax.fori_loop(0, groups, pack_parts, 0)
    exchange(part_out, part_in, 6)

    edge_copy.wait()
    last = row_iota(16)
    one16, two16 = masks[2, rows - 16 :, :], masks[3, rows - 16 :, :]
    first_one = jnp.where(last == 15, one16, 0.0)
    first_two = jnp.where(last == 14, two16, 0.0)
    second_two = jnp.where(last == 15, two16, 0.0)

    def finish(i, c):
        lanes = pl.ds(pl.multiple_of(i * LANES, LANES), LANES)
        one, two = taps[1:2, lanes], taps[2:3, lanes]
        e0, e1 = edge_in[0:1, lanes], edge_in[1:2, lanes]
        done = tail[:, lanes] + (first_one * one + first_two * two) * e0 + (second_two * two) * e1
        grad_feats[rows - 16 :, lanes] = done.astype(BF16)
        return c

    lax.fori_loop(0, 3 * groups, finish, 0)

    wait_all(part_in, 6, ctx - 1)

    def add_parts(k, acc):
        return acc + part_in[k]

    dp_out[...] = lax.fori_loop(0, ctx, add_parts, jnp.zeros((poles, LANES), F32))

    def send_dp(o, c):
        remote(dp_out, dp_in.at[my_dp], 7, {"dp": lax.rem(my_dp + o, dp)}).start()
        return c

    lax.fori_loop(1, dp, send_dp, 0)
    dp_in[pl.ds(my_dp, 1)] = dp_out[...][None]
    wait_all(dp_in, 7, dp - 1)
    whole = dp_in[0]
    for k in range(1, dp):
        whole = whole + dp_in[k]
    whole = whole * scale
    grad_res[...] = whole[:, : LANES // 2]
    turned = swap_halves(whole)
    grad_skip[...] = turned[9:10, : LANES // 2]
    tap_out[...] = jnp.where(lane_low(SUBS), turned[0:8], whole[8:16])

    def send_taps(o, c):
        remote(tap_out, tap_in.at[me], 8, {"ctx": peer_of(o)}).start()
        return c

    lax.fori_loop(1, ctx, send_taps, 0)
    tap_in[pl.ds(me, 1)] = tap_out[...][None]
    wait_all(tap_in, 8, ctx - 1)

    def place_taps(i, c):
        low, high = tap_in[2 * i], tap_in[2 * i + 1]
        first = join_pair(low, high, True)
        last_row = join_pair(low, high, False)[0:1]
        for third in range(3):
            for j in range(3):
                r = third * 3 + j
                grad_taps[j : j + 1, pl.ds(at(i, third), LANES)] = first[r : r + 1] if r < 8 else last_row
        return c

    lax.fori_loop(0, groups, place_taps, 0)

    wait_sent(params, 1, ctx - 1)
    wait_sent(skips, 2, ctx - 1)
    wait_sent(first_in, 3, ctx - 1)
    wait_sent(carry_in, 4, ctx - 1)
    wait_sent(part_in, 6, ctx - 1)
    wait_sent(dp_in, 7, dp - 1)
    wait_sent(tap_in, 8, ctx - 1)


def per_device(features, upstream, lengths, conv_taps, residues, log_rate, skip_gain):
    rows, width = features.shape[1:]
    channels = upstream.shape[2]
    poles = residues.shape[0]
    ctx = lax.axis_size("ctx")
    dp = lax.axis_size("dp")
    scale = 1.0 / math.sqrt(rows * ctx * dp)
    groups = channels // LANES
    own = jnp.concatenate([residues, log_rate], axis=1)
    own_skip = jnp.concatenate([skip_gain, skip_gain])[None]
    vmem = pl.BlockSpec(memory_space=pltpu.VMEM)
    smem = pl.BlockSpec(memory_space=pltpu.SMEM)
    slab = (ctx, poles, LANES)
    wide = pltpu.VMEM((rows * groups, LANES), F32)
    per_pole = pltpu.VMEM((poles * groups, LANES), F32)
    scratch = [
        pltpu.VMEM(slab, F32),
        pltpu.VMEM((ctx, 1, LANES), F32),
        pltpu.VMEM((SUBS, width), BF16),
        pltpu.VMEM(slab, BF16),
        pltpu.VMEM(slab, BF16),
        pltpu.VMEM(slab, BF16),
        pltpu.VMEM(slab, BF16),
        pltpu.VMEM(slab, F32),
        pltpu.VMEM(slab, F32),
        wide,
        wide,
        wide,
        wide,
        per_pole,
        per_pole,
        pltpu.VMEM((groups, LANES), F32),
        per_pole,
        per_pole,
        per_pole,
        pltpu.VMEM((groups, LANES), F32),
        pltpu.VMEM((8, rows, LANES), F32),
        pltpu.VMEM((2, width), F32),
        pltpu.VMEM((2, width), F32),
        pltpu.VMEM((16, width), F32),
        pltpu.VMEM((16, channels), F32),
        pltpu.VMEM(slab, F32),
        pltpu.VMEM(slab, F32),
        pltpu.VMEM((poles, LANES), F32),
        pltpu.VMEM((dp, poles, LANES), F32),
        pltpu.VMEM((SUBS, LANES), F32),
        pltpu.VMEM((ctx, SUBS, LANES), F32),
        pltpu.SemaphoreType.DMA((9,)),
        pltpu.SemaphoreType.DMA((9,)),
    ]
    grad_feats, grad_taps, grad_res, grad_skip = pl.pallas_call(
        functools.partial(kernel, ctx, dp, scale),
        out_shape=(
            jax.ShapeDtypeStruct((rows, width), BF16),
            jax.ShapeDtypeStruct((3, width), F32),
            jax.ShapeDtypeStruct(residues.shape, F32),
            jax.ShapeDtypeStruct((1, residues.shape[1]), F32),
        ),
        in_specs=[smem] + [vmem] * 5,
        out_specs=(vmem,) * 4,
        scratch_shapes=scratch,
        compiler_params=pltpu.CompilerParams(
            collective_id=0, has_side_effects=True, vmem_limit_bytes=48 * 1024 * 1024
        ),
        name="conv_block",
    )(lengths, features[0], upstream[0], conv_taps, own, own_skip)
    return (grad_feats[None], grad_taps, grad_res, grad_skip[0])


def solution(mesh):
    return jax.shard_map(
        per_device,
        mesh=mesh,
        in_specs=(
            P("dp", "ctx", None),
            P("dp", "ctx", None),
            P("dp", None),
            P(),
            P(None, "ctx"),
            P(None, "ctx"),
            P("ctx"),
        ),
        out_specs=(P("dp", "ctx", None), P(), P(None, "ctx"), P("ctx")),
        check_vma=False,
    )
```

time: 621 us -> 84.9 us (0.14); the launches traced: 610 us -> 84.6 us
  waiting for transfers between devices: 252 us -> 0 us
  local copies, waits for them, and re-layouts: 151 us -> 6.89 us
  Pallas kernels: 0 us -> 75.5 us
  other arithmetic: 67.8 us -> 1.59 us
  matrix products: 60.7 us -> 0 us
  starting transfers between devices: 46 us -> 0 us
  between operations: 15.7 us -> 0.65 us
  blocking collectives: 14.4 us -> 0 us
    psum x1 -> x0, waiting for transfers between devices: 234 us -> none  [per_device(): grad_taps = lax.psum(tap_sum, ('dp', 'ctx')) * grad_scale]
    pallas_call x0 -> x1, Pallas kernels: none -> 75.5 us  [per_device(): pl.pallas_call(functools.partial(kernel, ctx, dp, scale), out_shape=(jax....]
    dot_general x34 -> x0, matrix products: 60.7 us -> none  [the longest x8 27.9 us: group_fn(): jnp.einsum('pic,pimc->mc', other_blk, inner_state, precision=lax.Precisio...]
    all_to_all x4 -> x0, starting transfers between devices: 39.5 us -> none  [the longest x1 13.2 us: per_device(): lax.all_to_all(grad_out, 'ctx', split_axis=2, concat_axis=0, tiled=True)]
    dynamic_slice x40 -> x0, local copies, waits for them, and re-layouts: 22.3 us -> none  [modal_sweep(): lax.map(group_fn, (src_groups, seg_groups, other_groups))]
    slice x36 -> x0, local copies, waits for them, and re-layouts: 21.5 us -> none  [the longest x16 18.7 us: group_fn(): last_row = inner_state[:, -1]]
    dynamic_update_slice x65 -> x0, local copies, waits for them, and re-layouts: 18.8 us -> none  [the longest x64 18.4 us: modal_sweep(): lax.map(group_fn, (src_groups, seg_groups, other_groups))]
    rev x4 -> x0, local copies, waits for them, and re-layouts: 18.6 us -> none  [the longest x1 13.4 us: per_device(): gradf[::-1]]
  transfers between devices with their start and end apart: 7 -> 0, of which waited for: 5 -> 0; matrix products, arithmetic and copies ran while one was open for 10% -> 0% of each run, Pallas kernels for 0% -> 0%
where the time goes in v1:
time: 84.9 us; the launch traced here: 84.6 us
  Pallas kernels  75.5 us (89%)
  local copies, waits for them, and re-layouts  6.89 us (8%)
  other arithmetic  1.59 us (2%)
    pallas_call x1, Pallas kernels, per_device(): pl.pallas_call(functools.partial(kernel, ctx, dp, scale), out_shape=(jax....  75.5 us
    unnamed x12, local copies, waits for them, and re-layouts  6.89 us

profile of v1, /device:TPU:1, one launch (start us, length us, event | category | flops | bytes accessed | tf_op | source)
XLA Modules:
  0.0 84.6 jit_solution(3921341228995248889)
XLA Ops:
  0.6 0.8 maximum_bitcast_fusion.own_skip
  1.4 0.8 pad_maximum_fusion.own
  2.2 0.0 copy-start
  2.2 1.4 %copy-done = bf16[1,128,6144]{2,1,0:T(8,128)(2,1)S(1)} copy-done((bf16[1,128,6144]{2,1,0:T(8,128)(2,1)S(1)}, bf16[1,128,6144]{2,1,0:T(8,128)(2,1)}, u32[]{:S(2)}) %copy-start) | copy-done | bytes 1572888
  3.6 0.0 copy-start.1
  3.6 1.0 %copy-done.1 = bf16[1,128,2048]{2,1,0:T(8,128)(2,1)S(1)} copy-done((bf16[1,128,2048]{2,1,0:T(8,128)(2,1)S(1)}, bf16[1,128,2048]{2,1,0:T(8,128)(2,1)}, u32[]{:S(2)}) %copy-start.1) | copy-done | bytes 524312
  4.7 0.0 copy-start.2
  4.7 0.9 %copy-done.2 = f32[3,6144]{1,0:T(4,128)S(1)} copy-done((f32[3,6144]{1,0:T(4,128)S(1)}, f32[3,6144]{1,0:T(4,128)}, u32[]{:S(2)}) %copy-start.2) | copy-done | bytes 73752
  5.6 0.0 copy-start.3
  5.6 0.7 copy-done.3
  6.2 75.5 %conv_block.1 = (bf16[128,6144]{1,0:T(8,128)(2,1)S(1)}, f32[3,6144]{1,0:T(4,128)S(1)}, f32[16,64]{1,0:T(8,128)S(1)}, f32[1,64]{1,0:T(1,128)S(1)}) custom-call(s32[1,8]{1,0:T(1,128)S(1)} %copy-done.3, bf16[128,6144]{1,0:T(8,128)(2,1)S(1)} %bitcast.7, bf16[128,2048]{1,0:T(8,128)(2,1)S(1)} %bitcast.8, f32[3,6144]{1,0:T(4,128)S(1)} %copy-done.2, ...), custom_call_target="tpu_custom_call" | custom-call | tf_op jit(solution)/shard_map/conv_block/pallas_call | solution.py:505
  81.7 1.1 %copy.15 = bf16[1,128,6144]{2,1,0:T(8,128)(2,1)} copy(bf16[1,128,6144]{2,1,0:T(8,128)(2,1)S(1)} %bitcast.6) | data formatting | bytes 3145728
  82.9 0.6 copy.16
  83.5 0.6 copy.17
  84.1 0.5 copy.18
Async XLA Ops:
  2.2 1.4 %copy-start = (bf16[1,128,6144]{2,1,0:T(8,128)(2,1)S(1)}, bf16[1,128,6144]{2,1,0:T(8,128)(2,1)}, u32[]{:S(2)}) copy-start(bf16[1,128,6144]{2,1,0:T(8,128)(2,1)} %param.7) | copy-start | bytes 4718596
  3.6 1.0 %copy-start.1 = (bf16[1,128,2048]{2,1,0:T(8,128)(2,1)S(1)}, bf16[1,128,2048]{2,1,0:T(8,128)(2,1)}, u32[]{:S(2)}) copy-start(bf16[1,128,2048]{2,1,0:T(8,128)(2,1)} %param.8) | copy-start | bytes 1572868
  4.7 0.9 %copy-start.2 = (f32[3,6144]{1,0:T(4,128)S(1)}, f32[3,6144]{1,0:T(4,128)}, u32[]{:S(2)}) copy-start(f32[3,6144]{1,0:T(4,128)} %taps.1) | copy-start | bytes 221188
  5.6 0.7 copy-start.3

commit v2 on v1

v2 whole, which is shorter than its diff:
```python
import functools
import math

import jax
import jax.numpy as jnp
from jax import lax
from jax.experimental import pallas as pl
from jax.experimental.pallas import tpu as pltpu
from jax.sharding import PartitionSpec as P

MESH = pl.DeviceIdType.MESH
F32 = jnp.float32
BF16 = jnp.bfloat16
LANES = 128
SUBS = 8
GROUP = 4
NEAR = 4


def row_iota(rows):
    return lax.broadcasted_iota(jnp.int32, (rows, LANES), 0)


def lane_low(rows):
    return lax.broadcasted_iota(jnp.int32, (rows, LANES), 1) < LANES // 2


def swap_halves(x):
    return pltpu.roll(x, LANES // 2, 1)


def join_pair(low, high, first):
    mask = lane_low(low.shape[0])
    if first:
        return jnp.where(mask, low, swap_halves(high))
    return jnp.where(mask, swap_halves(low), high)


def split_pair(a, b):
    mask = lane_low(a.shape[0])
    return jnp.where(mask, a, swap_halves(b)), jnp.where(mask, swap_halves(a), b)


def unfold(low, high):
    return jnp.concatenate([join_pair(low, high, True), join_pair(low, high, False)], axis=0)


def fold(x):
    return jnp.where(lane_low(SUBS), x[:SUBS], swap_halves(x[SUBS:]))


def free_of(bounds, low, high):
    clear = None
    for bound in bounds:
        one = (low > bound) | (high < bound)
        clear = one if clear is None else clear & one
    return jnp.where(clear, 1.0, 0.0).astype(F32)


def kernel(
    ctx,
    dp,
    scale,
    lengths,
    feats_in,
    upstream_in,
    taps_in,
    res_in,
    rate_in,
    skip_in,
    grad_feats,
    grad_taps,
    grad_res,
    grad_skip,
    feats,
    upstream,
    taps,
    own_res,
    own_rate,
    own_skip,
    rate_out,
    res_out,
    skip_out,
    rates,
    residues,
    skips,
    halo,
    first_out,
    first_in,
    carry_out,
    carry_in,
    prefixes,
    joins,
    keeps,
    source,
    gradient,
    output,
    adjoint,
    keys,
    values,
    decay,
    coeff,
    powers,
    gain,
    state,
    costate,
    res_sum,
    skip_sum,
    masks,
    edge_out,
    edge_in,
    tail,
    res_part_out,
    res_part_in,
    res_dp_out,
    res_dp_in,
    part_out,
    part_in,
    dp_out,
    dp_in,
    tap_out,
    tap_in,
    load_sem,
    send_sem,
    recv_sem,
):
    rows, channels = upstream.shape
    poles = own_res.shape[0]
    groups = channels // LANES
    halves = groups // SUBS
    half_rows = rows * SUBS
    pole_rows = poles * SUBS
    steps = rows // SUBS
    window = rows * ctx
    me = lax.axis_index("ctx")
    my_dp = lax.axis_index("dp")

    def peer_of(o):
        return lax.rem(me + o, ctx)

    def dp_peer(o):
        return lax.rem(my_dp + o, dp)

    loads = [
        pltpu.make_async_copy(src, dst, load_sem.at[k])
        for k, (src, dst) in enumerate(
            [
                (rate_in, own_rate),
                (res_in, own_res),
                (skip_in, own_skip),
                (taps_in, taps),
                (feats_in, feats),
                (upstream_in, upstream),
            ]
        )
    ]
    for load in loads:
        load.start()
    barrier = pltpu.get_barrier_semaphore()

    def greet(o, c):
        pl.semaphore_signal(barrier, inc=1, device_id={"ctx": peer_of(o)}, device_id_type=MESH)
        return c

    lax.fori_loop(1, ctx, greet, 0)

    def greet_dp(o, c):
        pl.semaphore_signal(barrier, inc=1, device_id={"dp": dp_peer(o)}, device_id_type=MESH)
        return c

    lax.fori_loop(1, dp, greet_dp, 0)

    for load in loads[:3]:
        load.wait()
    rate_out[...] = jnp.concatenate([own_rate[:SUBS, :], own_rate[SUBS:, :]], axis=1)
    res_out[...] = jnp.concatenate([own_res[:SUBS, :], own_res[SUBS:, :]], axis=1)
    skip_out[...] = jnp.concatenate([own_skip[...], own_skip[...]], axis=1)

    bounds = [0]
    total = 0
    for j in range(lengths.shape[1] - 1):
        total = total + lengths[0, j]
        bounds.append(total)
    bounds.append(window)
    start = me * rows
    row = row_iota(rows)
    pos = start + row
    flat = 0 * row
    next_one = free_of(bounds, pos + 1, pos + 1)
    next_two = free_of(bounds, pos + 1, pos + 2)
    masks[0] = free_of(bounds, pos, pos)
    masks[1] = free_of(bounds, pos - 1, pos)
    masks[2] = next_one
    masks[3] = next_two

    pl.semaphore_wait(barrier, ctx - 1 + dp - 1)

    def remote(src, dst, k, to):
        return pltpu.make_async_remote_copy(
            src_ref=src, dst_ref=dst, send_sem=send_sem.at[k], recv_sem=recv_sem.at[k], device_id=to, device_id_type=MESH
        )

    halo_copy = remote(feats_in.at[pl.ds(rows - SUBS, SUBS)], halo, 0, {"ctx": peer_of(1)})
    halo_copy.start()

    def send_rates(o, c):
        remote(rate_out, rates.at[me], 1, {"ctx": peer_of(o)}).start()
        return c

    lax.fori_loop(1, ctx, send_rates, 0)

    def send_others(o, c):
        remote(res_out, residues.at[me], 2, {"ctx": peer_of(o)}).start()
        remote(skip_out, skips.at[me], 3, {"ctx": peer_of(o)}).start()
        return c

    lax.fori_loop(1, ctx, send_others, 0)
    rates[pl.ds(me, 1)] = rate_out[...][None]
    residues[pl.ds(me, 1)] = res_out[...][None]
    skips[pl.ds(me, 1)] = skip_out[...][None]

    masks[4] = free_of(bounds, pos + 1, flat + (start + rows - 1))
    masks[5] = free_of(bounds, flat + (start + 1), pos)
    masks[6] = jnp.where(row < rows - 1, next_one, 0.0)
    masks[7] = jnp.where(row < rows - 2, next_two, 0.0)
    masks[8] = free_of(bounds, flat + start, pos)
    masks[9] = free_of(bounds, pos + 1, flat + (start + rows))

    low16 = lane_low(poles)
    my_rate = jnp.concatenate([own_rate[...], own_rate[...]], axis=1)
    my_decay = jnp.exp(-jnp.exp(my_rate))
    block_decay = jnp.exp(-jnp.exp(my_rate) * rows)

    def join_masks(k, c):
        low = jnp.where(low16, k * rows, (ctx - 1 - k) * rows + 1)
        joins[k] = free_of(bounds, low, low + (rows - 1)) * block_decay
        keeps[k] = free_of(bounds, low, low) * my_decay
        return c

    lax.fori_loop(0, ctx, join_masks, 0)

    my_y, my_z = lax.div(me, 2 * NEAR), lax.rem(lax.div(me, 2), NEAR)

    def group_of(s):
        b, t = lax.div(s, NEAR), lax.rem(s, NEAR)
        upper = lax.div(b, 2)
        z_off = (1 - upper) * (b + 2) + upper * (3 - b)
        y = lax.rem(my_y + t + 2, NEAR)
        return y * NEAR + lax.rem(my_z + z_off, NEAR)

    def at(i, third):
        return pl.multiple_of(third * channels + i * LANES, LANES)

    def strided(s, count, stride_rows):
        return pl.ds(lax.div(s, SUBS) * stride_rows + lax.rem(s, SUBS), count, stride=SUBS)

    for load in loads[3:]:
        load.wait()
    halo_copy.wait()

    def featured(off):
        lanes = pl.ds(off, LANES)
        f = feats[:, lanes].astype(F32)
        ext = jnp.concatenate([halo[:, lanes].astype(F32), f], axis=0)
        one = masks[0] * pltpu.roll(ext, 1, 0)[SUBS:]
        two = masks[1] * pltpu.roll(ext, 2, 0)[SUBS:]
        return taps[0:1, lanes] * f + taps[1:2, lanes] * one + taps[2:3, lanes] * two

    def enter(s, c):
        i = group_of(s)
        query, key, value = (featured(at(i, third)) for third in range(3))
        lanes = pl.ds(at(i, 0), LANES)
        up = upstream[:, lanes].astype(F32)
        keys[:, lanes] = key
        values[:, lanes] = value
        source[strided(s, rows, half_rows), :] = (key * value).astype(BF16).astype(F32)
        gradient[strided(s, rows, half_rows), :] = (up * query).astype(BF16).astype(F32)
        return c

    lax.fori_loop(0, groups, enter, 0)

    def all_slots(buf, sem, slots):
        pltpu.make_async_copy(buf.at[pl.ds(0, slots)], buf.at[pl.ds(0, slots)], sem).wait()

    def wait_all(buf, k, slots):
        all_slots(buf, recv_sem.at[k], slots)

    wait_all(rates, 1, ctx - 1)

    def spread_rates(s, c):
        i = group_of(s)
        decay[strided(s, poles, pole_rows), :] = jnp.exp(-jnp.exp(unfold(rates[2 * i], rates[2 * i + 1])))
        return c

    lax.fori_loop(0, groups, spread_rates, 0, unroll=True)

    def send_slab(out, into, k, to):
        @pl.when(to != me)
        def _():
            remote(out.at[to], into.at[me], k, {"ctx": to}).start()

        @pl.when(to == me)
        def _():
            into[pl.ds(me, 1)] = out[pl.ds(me, 1)]

    def send_slots(out, into, k, low, high):
        def send(s, c):
            i = group_of(s)
            send_slab(out, into, k, 2 * i)
            send_slab(out, into, k, 2 * i + 1)
            return c

        lax.fori_loop(low, high, send, 0)

    for h in range(halves):
        pole_at = pl.ds(h * pole_rows, pole_rows)
        fac = decay[pole_at, :].reshape(poles, SUBS, LANES)

        def chunk(k, carry):
            s, u = carry
            back = steps - 1 - k
            x = source[pl.ds(pl.multiple_of(h * half_rows + k * 64, 64), 64), :].reshape(SUBS, SUBS, LANES)
            g = gradient[pl.ds(pl.multiple_of(h * half_rows + back * 64, 64), 64), :].reshape(SUBS, SUBS, LANES)
            mx = masks[4, pl.ds(pl.multiple_of(k * SUBS, SUBS), SUBS), :]
            mg = masks[5, pl.ds(pl.multiple_of(back * SUBS, SUBS), SUBS), :]
            for t in range(SUBS):
                r = SUBS - 1 - t
                s = s * fac + (x[t] * mx[t : t + 1])[None]
                u = u * fac + (g[r] * mg[r : r + 1])[None]
            return s, u

        zero = jnp.zeros((poles, SUBS, LANES), F32)
        s, u = lax.fori_loop(0, steps, chunk, (zero, zero))
        state[pole_at, :] = s.reshape(pole_rows, LANES)
        costate[pole_at, :] = u.reshape(pole_rows, LANES)

        def pack_first(s, c):
            i = group_of(s)
            low, high = split_pair(state[strided(s, poles, pole_rows), :], costate[strided(s, poles, pole_rows), :])
            first_out[2 * i] = low.astype(BF16)
            first_out[2 * i + 1] = high.astype(BF16)
            return c

        lax.fori_loop(h * SUBS, (h + 1) * SUBS, pack_first, 0, unroll=True)
        send_slots(first_out, first_in, 4, h * SUBS, (h + 1) * SUBS)

    wait_all(residues, 2, ctx - 1)
    wait_all(skips, 3, ctx - 1)

    def spread_others(s, c):
        i = group_of(s)
        coeff[strided(s, poles, pole_rows), :] = unfold(residues[2 * i], residues[2 * i + 1])
        low_s = jnp.broadcast_to(skips[2 * i], (SUBS, LANES))
        high_s = jnp.broadcast_to(skips[2 * i + 1], (SUBS, LANES))
        gain[pl.ds(s, 1), :] = join_pair(low_s, high_s, True)[0:1]
        return c

    lax.fori_loop(0, groups, spread_others, 0, unroll=True)
    state[...] = jnp.zeros_like(state)
    costate[...] = jnp.zeros_like(costate)
    res_sum[...] = jnp.zeros_like(res_sum)
    skip_sum[...] = jnp.zeros_like(skip_sum)

    def raise_powers(h):
        pole_at = pl.ds(h * pole_rows, pole_rows)
        fac = decay[pole_at, :].reshape(poles, SUBS, LANES)

        def step(k, e):
            for t in range(4):
                e = e * fac
                to = pl.multiple_of((h * rows + k * 4 + t) * pole_rows, pole_rows)
                powers[pl.ds(to, pole_rows), :] = e.reshape(pole_rows, LANES)
            return e

        lax.fori_loop(0, rows // 4, step, coeff[pole_at, :].reshape(poles, SUBS, LANES))

    def half_sweep(h):
        both = pl.ds(h * SUBS, SUBS)
        skip = gain[both, :]

        def chunk(k, c):
            back = steps - 1 - k
            at_x = pl.ds(pl.multiple_of(h * half_rows + k * 64, 64), 64)
            at_g = pl.ds(pl.multiple_of(h * half_rows + back * 64, 64), 64)
            x = source[at_x, :].reshape(SUBS, SUBS, LANES)
            gx = gradient[at_x, :].reshape(SUBS, SUBS, LANES)
            g = gradient[at_g, :].reshape(SUBS, SUBS, LANES)
            keep = masks[0, pl.ds(pl.multiple_of(k * SUBS, SUBS), SUBS), :]
            keep_g = masks[2, pl.ds(pl.multiple_of(back * SUBS, SUBS), SUBS), :]
            out = [skip * x[t] for t in range(SUBS)]
            adj = [skip * g[t] for t in range(SUBS)]
            for p in range(0, poles, GROUP):
                here = pl.ds(h * pole_rows + p * SUBS, GROUP * SUBS)
                shape = (GROUP, SUBS, LANES)
                s = state[here, :].reshape(shape)
                u = costate[here, :].reshape(shape)
                fac = decay[here, :].reshape(shape)
                res = coeff[here, :].reshape(shape)
                acc = res_sum[here, :].reshape(shape)
                for t in range(SUBS):
                    r = SUBS - 1 - t
                    s = s * (fac * keep[t : t + 1][None]) + x[t][None]
                    out[t] = out[t] + jnp.sum(res * s, axis=0)
                    acc = acc + s * gx[t][None]
                    u = u * (fac * keep_g[r : r + 1][None]) + g[r][None]
                    adj[r] = adj[r] + jnp.sum(res * u, axis=0)
                state[here, :] = s.reshape(GROUP * SUBS, LANES)
                costate[here, :] = u.reshape(GROUP * SUBS, LANES)
                res_sum[here, :] = acc.reshape(GROUP * SUBS, LANES)
            output[at_x, :] = jnp.stack(out).reshape(SUBS * SUBS, LANES)
            adjoint[at_g, :] = jnp.stack(adj).reshape(SUBS * SUBS, LANES)
            skip_sum[both, :] = skip_sum[both, :] + jnp.sum(x * gx, axis=0)
            return c

        lax.fori_loop(0, steps, chunk, 0)

    raise_powers(0)
    half_sweep(0)

    wait_all(first_in, 4, ctx - 1)

    def scan(k, w):
        prefixes[k] = w
        here = jnp.where(low16, first_in[k].astype(F32), first_in[ctx - 1 - k].astype(F32))
        return joins[k] * w + here

    lax.fori_loop(0, ctx, scan, jnp.zeros((poles, LANES), F32), unroll=True)

    def pack_carry(k, c):
        carry_out[k] = jnp.where(low16, prefixes[k], prefixes[ctx - 1 - k]).astype(BF16)
        return c

    lax.fori_loop(0, ctx, pack_carry, 0, unroll=True)
    send_slots(carry_out, carry_in, 5, 0, groups)

    raise_powers(1)
    half_sweep(1)

    def pack_res(s, c):
        i = group_of(s)
        a = res_sum[strided(s, poles, pole_rows), :]
        low, high = split_pair(a[:SUBS], a[SUBS:])
        res_part_out[2 * i] = low
        res_part_out[2 * i + 1] = high
        return c

    lax.fori_loop(0, groups, pack_res, 0, unroll=True)
    send_slots(res_part_out, res_part_in, 6, 0, groups)

    def carried_terms(k, acc):
        return acc + keeps[k] * prefixes[k] * swap_halves(first_in[k].astype(F32))

    res_carried = fold(lax.fori_loop(0, ctx, carried_terms, jnp.zeros((poles, LANES), F32)))

    wait_all(carry_in, 5, ctx - 1)

    def unpack_carry(s, c):
        i = group_of(s)
        low, high = carry_in[2 * i].astype(F32), carry_in[2 * i + 1].astype(F32)
        state[strided(s, poles, pole_rows), :] = join_pair(low, high, True)
        costate[strided(s, poles, pole_rows), :] = join_pair(low, high, False)
        return c

    lax.fori_loop(0, groups, unpack_carry, 0, unroll=True)

    for h in range(halves):
        pole_at = pl.ds(h * pole_rows, pole_rows)
        s = state[pole_at, :].reshape(poles, SUBS, LANES)
        u = costate[pole_at, :].reshape(poles, SUBS, LANES)

        def add_carry(k, c):
            for j in range(4):
                t = k * 4 + j
                r = rows - 1 - t
                e = powers[pl.ds(pl.multiple_of((h * rows + t) * pole_rows, pole_rows), pole_rows), :]
                e = e.reshape(poles, SUBS, LANES)
                at_t = pl.ds(pl.multiple_of(h * half_rows + t * SUBS, SUBS), SUBS)
                at_r = pl.ds(pl.multiple_of(h * half_rows + r * SUBS, SUBS), SUBS)
                output[at_t, :] = output[at_t, :] + masks[8, pl.ds(t, 1), :] * jnp.sum(e * s, axis=0)
                adjoint[at_r, :] = adjoint[at_r, :] + masks[9, pl.ds(r, 1), :] * jnp.sum(e * u, axis=0)
            return c

        lax.fori_loop(0, rows // 4, add_carry, 0)

    first_keep, first_both, second_both = masks[0, 0:1, :], masks[1, 0:1, :], masks[1, 1:2, :]

    def leave(s, c):
        i = group_of(s)
        here = pl.ds(at(i, 0), LANES)
        out = output[strided(s, rows, half_rows), :].astype(BF16).astype(F32)
        mixed = adjoint[strided(s, rows, half_rows), :].astype(BF16).astype(F32)
        up = upstream[:, here].astype(F32)
        sums = []
        for third, post in enumerate((up * out, mixed * values[:, here], mixed * keys[:, here])):
            lanes = pl.ds(at(i, third), LANES)
            f = feats[:, lanes].astype(F32)
            before = halo[:, lanes].astype(F32)
            one = masks[6] * pltpu.roll(post, rows - 1, 0)
            two = masks[7] * pltpu.roll(post, rows - 2, 0)
            p0, p1 = post[0:1], post[1:2]
            h1, h2 = before[SUBS - 1 :], before[SUBS - 2 : SUBS - 1]
            sums.append(jnp.sum(post * f, axis=0, keepdims=True))
            sums.append(jnp.sum(one * f, axis=0, keepdims=True) + p0 * first_keep * h1)
            sums.append(jnp.sum(two * f, axis=0, keepdims=True) + p0 * first_both * h2 + p1 * second_both * h1)
            edge_out[:, lanes] = post[0:2]
            back = taps[0:1, lanes] * post + taps[1:2, lanes] * one + taps[2:3, lanes] * two
            grad_feats[:, lanes] = back.astype(BF16)
            tail[:, lanes] = back[rows - 16 :]
        top = jnp.concatenate(sums[:SUBS], axis=0)
        rest = jnp.concatenate([sums[SUBS], skip_sum[pl.ds(s, 1), :]] + sums[:6], axis=0)
        low, high = split_pair(top, rest)
        part_out[2 * i] = low
        part_out[2 * i + 1] = high

        @pl.when(s > 0)
        def _():
            j = group_of(s - 1)
            send_slab(part_out, part_in, 9, 2 * j)
            send_slab(part_out, part_in, 9, 2 * j + 1)

        return c

    lax.fori_loop(0, groups, leave, 0)
    edge_copy = remote(edge_out, edge_in, 8, {"ctx": peer_of(ctx - 1)})
    edge_copy.start()
    send_slots(part_out, part_in, 9, groups - 1, groups)

    def sum_slots(buf, count):
        return lax.fori_loop(0, count, lambda k, acc: acc + buf[k], jnp.zeros((SUBS, LANES), F32), unroll=True)

    wait_all(res_part_in, 6, ctx - 1)
    res_dp_out[...] = sum_slots(res_part_in, ctx) + res_carried

    def send_res(o, c):
        remote(res_dp_out, res_dp_in.at[my_dp], 7, {"dp": dp_peer(o)}).start()
        return c

    lax.fori_loop(1, dp, send_res, 0)
    res_dp_in[pl.ds(my_dp, 1)] = res_dp_out[...][None]

    edge_copy.wait()
    last = row_iota(16)
    one16, two16 = masks[2, rows - 16 :, :], masks[3, rows - 16 :, :]
    first_one = jnp.where(last == 15, one16, 0.0)
    first_two = jnp.where(last == 14, two16, 0.0)
    second_two = jnp.where(last == 15, two16, 0.0)

    def finish(i, c):
        lanes = pl.ds(pl.multiple_of(i * LANES, LANES), LANES)
        one, two = taps[1:2, lanes], taps[2:3, lanes]
        e0, e1 = edge_in[0:1, lanes], edge_in[1:2, lanes]
        done = tail[:, lanes] + (first_one * one + first_two * two) * e0 + (second_two * two) * e1
        grad_feats[rows - 16 :, lanes] = done.astype(BF16)
        return c

    wait_all(part_in, 9, ctx - 1)
    dp_out[...] = sum_slots(part_in, ctx)

    def send_dp(o, c):
        remote(dp_out, dp_in.at[my_dp], 10, {"dp": dp_peer(o)}).start()
        return c

    lax.fori_loop(1, dp, send_dp, 0)
    dp_in[pl.ds(my_dp, 1)] = dp_out[...][None]
    wait_all(dp_in, 10, dp - 1)
    whole = sum_slots(dp_in, dp) * scale
    tap_out[...] = whole

    def send_taps(o, c):
        remote(tap_out, tap_in.at[me], 11, {"ctx": peer_of(o)}).start()
        return c

    lax.fori_loop(1, ctx, send_taps, 0)
    tap_in[pl.ds(me, 1)] = whole[None]
    grad_skip[...] = swap_halves(whole)[1:2, : LANES // 2]

    lax.fori_loop(0, 3 * groups, finish, 0)
    wait_all(res_dp_in, 7, dp - 1)
    res_whole = sum_slots(res_dp_in, dp) * scale
    grad_res[:SUBS, :] = res_whole[:, : LANES // 2]
    grad_res[SUBS:, :] = swap_halves(res_whole)[:, : LANES // 2]
    for k, buf, slots in [
        (1, rates, ctx),
        (2, residues, ctx),
        (3, skips, ctx),
        (4, first_in, ctx),
        (5, carry_in, ctx),
        (6, res_part_in, ctx),
        (7, res_dp_in, dp),
        (9, part_in, ctx),
        (10, dp_in, dp),
        (11, tap_in, ctx),
    ]:
        all_slots(buf, send_sem.at[k], slots - 1)

    wait_all(tap_in, 11, ctx - 1)

    def place_taps(i, c):
        low, high = tap_in[2 * i], tap_in[2 * i + 1]
        first = join_pair(low, high, True)
        last_row = join_pair(low, high, False)[0:1]
        for third in range(3):
            for j in range(3):
                r = third * 3 + j
                grad_taps[j : j + 1, pl.ds(at(i, third), LANES)] = first[r : r + 1] if r < SUBS else last_row
        return c

    lax.fori_loop(0, groups, place_taps, 0, unroll=True)


def per_device(features, upstream, lengths, conv_taps, residues, log_rate, skip_gain):
    rows, width = features.shape[1:]
    channels = upstream.shape[2]
    poles, owned = residues.shape
    ctx = lax.axis_size("ctx")
    dp = lax.axis_size("dp")
    scale = 1.0 / math.sqrt(rows * ctx * dp)
    groups = channels // LANES
    vmem = pl.BlockSpec(memory_space=pltpu.VMEM)
    smem = pl.BlockSpec(memory_space=pltpu.SMEM)
    hbm = pl.BlockSpec(memory_space=pltpu.HBM)
    slab = (ctx, poles, LANES)
    folded = (ctx, SUBS, LANES)
    wide = pltpu.VMEM((rows * groups, LANES), F32)
    per_pole = pltpu.VMEM((poles * groups, LANES), F32)
    scratch = [
        pltpu.VMEM((rows, width), BF16),
        pltpu.VMEM((rows, channels), BF16),
        pltpu.VMEM((3, width), F32),
        pltpu.VMEM((poles, owned), F32),
        pltpu.VMEM((poles, owned), F32),
        pltpu.VMEM((1, owned), F32),
        pltpu.VMEM((SUBS, LANES), F32),
        pltpu.VMEM((SUBS, LANES), F32),
        pltpu.VMEM((1, LANES), F32),
        pltpu.VMEM(folded, F32),
        pltpu.VMEM(folded, F32),
        pltpu.VMEM((ctx, 1, LANES), F32),
        pltpu.VMEM((SUBS, width), BF16),
        pltpu.VMEM(slab, BF16),
        pltpu.VMEM(slab, BF16),
        pltpu.VMEM(slab, BF16),
        pltpu.VMEM(slab, BF16),
        pltpu.VMEM(slab, F32),
        pltpu.VMEM(slab, F32),
        pltpu.VMEM(slab, F32),
        wide,
        wide,
        wide,
        wide,
        pltpu.VMEM((rows, channels), F32),
        pltpu.VMEM((rows, channels), F32),
        per_pole,
        per_pole,
        pltpu.VMEM((rows * poles * groups, LANES), F32),
        pltpu.VMEM((groups, LANES), F32),
        per_pole,
        per_pole,
        per_pole,
        pltpu.VMEM((groups, LANES), F32),
        pltpu.VMEM((10, rows, LANES), F32),
        pltpu.VMEM((2, width), F32),
        pltpu.VMEM((2, width), F32),
        pltpu.VMEM((16, width), F32),
        pltpu.VMEM(folded, F32),
        pltpu.VMEM(folded, F32),
        pltpu.VMEM((SUBS, LANES), F32),
        pltpu.VMEM((dp, SUBS, LANES), F32),
        pltpu.VMEM(folded, F32),
        pltpu.VMEM(folded, F32),
        pltpu.VMEM((SUBS, LANES), F32),
        pltpu.VMEM((dp, SUBS, LANES), F32),
        pltpu.VMEM((SUBS, LANES), F32),
        pltpu.VMEM(folded, F32),
        pltpu.SemaphoreType.DMA((6,)),
        pltpu.SemaphoreType.DMA((12,)),
        pltpu.SemaphoreType.DMA((12,)),
    ]
    grad_feats, grad_taps, grad_res, grad_skip = pl.pallas_call(
        functools.partial(kernel, ctx, dp, scale),
        out_shape=(
            jax.ShapeDtypeStruct((rows, width), BF16),
            jax.ShapeDtypeStruct((3, width), F32),
            jax.ShapeDtypeStruct((poles, owned), F32),
            jax.ShapeDtypeStruct((1, owned), F32),
        ),
        in_specs=[smem] + [hbm] * 6,
        out_specs=(vmem,) * 4,
        scratch_shapes=scratch,
        compiler_params=pltpu.CompilerParams(
            collective_id=0, has_side_effects=True, vmem_limit_bytes=56 * 1024 * 1024
        ),
        name="conv_block",
    )(lengths, features[0], upstream[0], conv_taps, residues, log_rate, skip_gain[None])
    return (grad_feats[None], grad_taps, grad_res, grad_skip[0])


def solution(mesh):
    return jax.shard_map(
        per_device,
        mesh=mesh,
        in_specs=(
            P("dp", "ctx", None),
            P("dp", "ctx", None),
            P("dp", None),
            P(),
            P(None, "ctx"),
            P(None, "ctx"),
            P("ctx"),
        ),
        out_specs=(P("dp", "ctx", None), P(), P(None, "ctx"), P("ctx")),
        check_vma=False,
    )
```

time: 84.9 us -> 68.4 us (0.81)
  Pallas kernels: 75.5 us -> 63.1 us
  local copies, waits for them, and re-layouts: 6.89 us -> 4.49 us
  other arithmetic: 1.59 us -> 0 us
    pallas_call x1, Pallas kernels: 75.5 us -> 63.1 us  [per_device(): pl.pallas_call(functools.partial(kernel, ctx, dp, scale), out_shape=(jax....]
    unnamed x12 -> x10, local copies, waits for them, and re-layouts: 6.89 us -> 4.49 us
where the time goes in v2:
time: 68.4 us; the launch traced here: 68.3 us
  Pallas kernels  63.1 us (92%)
  local copies, waits for them, and re-layouts  4.49 us (7%)
    pallas_call x1, Pallas kernels, per_device(): pl.pallas_call(functools.partial(kernel, ctx, dp, scale), out_shape=(jax....  63.1 us
    unnamed x10, local copies, waits for them, and re-layouts  4.49 us

profile of v2, /device:TPU:1, one launch (start us, length us, event | category | flops | bytes accessed | tf_op | source)
XLA Modules:
  0.0 68.3 jit_solution(7200051306074296776)
XLA Ops:
  0.6 63.1 %conv_block.1 = (bf16[128,6144]{1,0:T(8,128)(2,1)}, f32[3,6144]{1,0:T(4,128)}, f32[16,64]{1,0:T(8,128)}, f32[1,64]{1,0:T(1,128)}) custom-call(s32[1,8]{1,0:T(1,128)} %lengths.1, bf16[128,6144]{1,0:T(8,128)(2,1)} %bitcast.6, bf16[128,2048]{1,0:T(8,128)(2,1)} %bitcast.7, f32[3,6144]{1,0:T(4,128)} %taps_in.1, f32[16,64]{1,0:T(8,128)} %res_in.1, ...), custom_call_target="tpu_custom_call" | custom-call | tf_op jit(solution)/shard_map/conv_block/pallas_call | solution.py:679
  63.8 0.0 copy-start
  63.8 0.0 copy-start.1
  63.8 0.0 copy-start.2
  63.8 2.7 %copy.15 = bf16[1,128,6144]{2,1,0:T(8,128)(2,1)} copy(bf16[1,128,6144]{2,1,0:T(8,128)(2,1)} %bitcast.5) | data formatting | bytes 3145728
  66.5 0.0 copy-done
  66.5 0.6 copy.16
  67.2 0.0 copy-done.1
  67.2 0.6 copy.17
  67.8 0.0 copy-done.2
  67.8 0.5 copy.18
Async XLA Ops:
  63.8 2.8 %copy-start = (f32[3,6144]{1,0:T(4,128)S(1)}, f32[3,6144]{1,0:T(4,128)}, u32[]{:S(2)}) copy-start(f32[3,6144]{1,0:T(4,128)} %get-tuple-element.17) | copy-start | bytes 221188
  63.8 3.4 %copy-start.1 = (f32[16,64]{1,0:T(8,128)S(1)}, f32[16,64]{1,0:T(8,128)}, u32[]{:S(2)}) copy-start(f32[16,64]{1,0:T(8,128)} %get-tuple-element.18) | copy-start | bytes 12292
  63.8 4.0 %copy-start.2 = (f32[1,64]{1,0:T(1,128)S(1)}, f32[1,64]{1,0:T(1,128)}, u32[]{:S(2)}) copy-start(f32[1,64]{1,0:T(1,128)} %get-tuple-element.11) | copy-start | bytes 772

commit v3 on v2

--- a/solution.py
+++ b/solution.py
@@ -84,6 +84,7 @@
     rates,
     residues,
     skips,
+    halo_out,
     halo,
     first_out,
     first_in,
@@ -96,6 +97,7 @@
     gradient,
     output,
     adjoint,
+    queries,
     keys,
     values,
     decay,
@@ -138,6 +140,13 @@
     def peer_of(o):
         return lax.rem(me + o, ctx)
 
+    def far_first(o):
+        k, j = lax.div(o, 4), lax.rem(o, 4)
+        z_off = 4 + (1 - 2 * lax.rem(k, 2)) * lax.div(k + 1, 2)
+        y_off = 2 + (1 - 2 * lax.rem(j, 2)) * lax.div(j + 1, 2)
+        y = lax.rem(lax.div(me, 8) + y_off, 4)
+        return y * 8 + lax.rem(lax.rem(me, 8) + z_off, 8)
+
     def dp_peer(o):
         return lax.rem(my_dp + o, dp)
 
@@ -193,38 +202,14 @@
     masks[2] = next_one
     masks[3] = next_two
 
-    pl.semaphore_wait(barrier, ctx - 1 + dp - 1)
-
-    def remote(src, dst, k, to):
-        return pltpu.make_async_remote_copy(
-            src_ref=src, dst_ref=dst, send_sem=send_sem.at[k], recv_sem=recv_sem.at[k], device_id=to, device_id_type=MESH
-        )
-
-    halo_copy = remote(feats_in.at[pl.ds(rows - SUBS, SUBS)], halo, 0, {"ctx": peer_of(1)})
-    halo_copy.start()
-
-    def send_rates(o, c):
-        remote(rate_out, rates.at[me], 1, {"ctx": peer_of(o)}).start()
-        return c
-
-    lax.fori_loop(1, ctx, send_rates, 0)
-
-    def send_others(o, c):
-        remote(res_out, residues.at[me], 2, {"ctx": peer_of(o)}).start()
-        remote(skip_out, skips.at[me], 3, {"ctx": peer_of(o)}).start()
-        return c
-
-    lax.fori_loop(1, ctx, send_others, 0)
-    rates[pl.ds(me, 1)] = rate_out[...][None]
-    residues[pl.ds(me, 1)] = res_out[...][None]
-    skips[pl.ds(me, 1)] = skip_out[...][None]
-
     masks[4] = free_of(bounds, pos + 1, flat + (start + rows - 1))
     masks[5] = free_of(bounds, flat + (start + 1), pos)
     masks[6] = jnp.where(row < rows - 1, next_one, 0.0)
     masks[7] = jnp.where(row < rows - 2, next_two, 0.0)
     masks[8] = free_of(bounds, flat + start, pos)
     masks[9] = free_of(bounds, pos + 1, flat + (start + rows))
+    masks[10] = jnp.where(row > 0, masks[0], 0.0)
+    masks[11] = jnp.where(row > 1, masks[1], 0.0)
 
     low16 = lane_low(poles)
     my_rate = jnp.concatenate([own_rate[...], own_rate[...]], axis=1)
@@ -256,14 +241,13 @@
 
     for load in loads[3:]:
         load.wait()
-    halo_copy.wait()
 
     def featured(off):
         lanes = pl.ds(off, LANES)
         f = feats[:, lanes].astype(F32)
-        ext = jnp.concatenate([halo[:, lanes].astype(F32), f], axis=0)
-        one = masks[0] * pltpu.roll(ext, 1, 0)[SUBS:]
-        two = masks[1] * pltpu.roll(ext, 2, 0)[SUBS:]
+        one = masks[10] * pltpu.roll(f, 1, 0)
+        two = masks[11] * pltpu.roll(f, 2, 0)
+        halo_out[:, lanes] = f[rows - 2 :]
         return taps[0:1, lanes] * f + taps[1:2, lanes] * one + taps[2:3, lanes] * two
 
     def enter(s, c):
@@ -273,11 +257,62 @@
         up = upstream[:, lanes].astype(F32)
         keys[:, lanes] = key
         values[:, lanes] = value
+        queries[:, lanes] = query[:SUBS]
         source[strided(s, rows, half_rows), :] = (key * value).astype(BF16).astype(F32)
         gradient[strided(s, rows, half_rows), :] = (up * query).astype(BF16).astype(F32)
         return c
 
     lax.fori_loop(0, groups, enter, 0)
+
+    pl.semaphore_wait(barrier, ctx - 1 + dp - 1)
+
+    def remote(src, dst, k, to):
+        return pltpu.make_async_remote_copy(
+            src_ref=src, dst_ref=dst, send_sem=send_sem.at[k], recv_sem=recv_sem.at[k], device_id=to, device_id_type=MESH
+        )
+
+    def send_rates(o, c):
+        remote(rate_out, rates.at[me], 1, {"ctx": far_first(o)}).start()
+        return c
+
+    lax.fori_loop(0, ctx - 1, send_rates, 0)
+    halo_copy = remote(halo_out, halo, 0, {"ctx": peer_of(1)})
+    halo_copy.start()
+
+    def send_others(o, c):
+        remote(res_out, residues.at[me], 2, {"ctx": far_first(o)}).start()
+        remote(skip_out, skips.at[me], 3, {"ctx": far_first(o)}).start()
+        return c
+
+    lax.fori_loop(0, ctx - 1, send_others, 0)
+    rates[pl.ds(me, 1)] = rate_out[...][None]
+    residues[pl.ds(me, 1)] = res_out[...][None]
+    skips[pl.ds(me, 1)] = skip_out[...][None]
+
+    halo_copy.wait()
+    head = row_iota(SUBS)
+    on_first = jnp.where(head == 0, masks[0, :SUBS, :], 0.0)
+    both_first = jnp.where(head == 0, masks[1, :SUBS, :], 0.0)
+    both_second = jnp.where(head == 1, masks[1, :SUBS, :], 0.0)
+
+    def mend(s, c):
+        i = group_of(s)
+        here = pl.ds(at(i, 0), LANES)
+        parts = []
+        for third, buf in enumerate((queries, keys, values)):
+            lanes = pl.ds(at(i, third), LANES)
+            one, two = taps[1:2, lanes], taps[2:3, lanes]
+            h1, h2 = halo[1:2, lanes], halo[0:1, lanes]
+            parts.append(buf[:SUBS, here] + (on_first * one + both_second * two) * h1 + (both_first * two) * h2)
+        query, key, value = parts
+        keys[:SUBS, here] = key
+        values[:SUBS, here] = value
+        up = upstream[: 2 * SUBS, here].astype(F32)[:SUBS]
+        source[strided(s, SUBS, half_rows), :] = (key * value).astype(BF16).astype(F32)
+        gradient[strided(s, SUBS, half_rows), :] = (up * query).astype(BF16).astype(F32)
+        return c
+
+    lax.fori_loop(0, groups, mend, 0, unroll=True)
 
     def all_slots(buf, sem, slots):
         pltpu.make_async_copy(buf.at[pl.ds(0, slots)], buf.at[pl.ds(0, slots)], sem).wait()
@@ -416,6 +451,7 @@
 
     raise_powers(0)
     half_sweep(0)
+    raise_powers(1)
 
     wait_all(first_in, 4, ctx - 1)
 
@@ -433,7 +469,6 @@
     lax.fori_loop(0, ctx, pack_carry, 0, unroll=True)
     send_slots(carry_out, carry_in, 5, 0, groups)
 
-    raise_powers(1)
     half_sweep(1)
 
     def pack_res(s, c):
@@ -494,11 +529,10 @@
         for third, post in enumerate((up * out, mixed * values[:, here], mixed * keys[:, here])):
             lanes = pl.ds(at(i, third), LANES)
             f = feats[:, lanes].astype(F32)
-            before = halo[:, lanes].astype(F32)
             one = masks[6] * pltpu.roll(post, rows - 1, 0)
             two = masks[7] * pltpu.roll(post, rows - 2, 0)
             p0, p1 = post[0:1], post[1:2]
-            h1, h2 = before[SUBS - 1 :], before[SUBS - 2 : SUBS - 1]
+            h1, h2 = halo[1:2, lanes], halo[0:1, lanes]
             sums.append(jnp.sum(post * f, axis=0, keepdims=True))
             sums.append(jnp.sum(one * f, axis=0, keepdims=True) + p0 * first_keep * h1)
             sums.append(jnp.sum(two * f, axis=0, keepdims=True) + p0 * first_both * h2 + p1 * second_both * h1)
@@ -528,6 +562,15 @@
     def sum_slots(buf, count):
         return lax.fori_loop(0, count, lambda k, acc: acc + buf[k], jnp.zeros((SUBS, LANES), F32), unroll=True)
 
+    wait_all(part_in, 9, ctx - 1)
+    dp_out[...] = sum_slots(part_in, ctx)
+
+    def send_dp(o, c):
+        remote(dp_out, dp_in.at[my_dp], 10, {"dp": dp_peer(o)}).start()
+        return c
+
+    lax.fori_loop(1, dp, send_dp, 0)
+    dp_in[pl.ds(my_dp, 1)] = dp_out[...][None]
     wait_all(res_part_in, 6, ctx - 1)
     res_dp_out[...] = sum_slots(res_part_in, ctx) + res_carried
 
@@ -537,6 +580,17 @@
 
     lax.fori_loop(1, dp, send_res, 0)
     res_dp_in[pl.ds(my_dp, 1)] = res_dp_out[...][None]
+    wait_all(dp_in, 10, dp - 1)
+    whole = sum_slots(dp_in, dp) * scale
+    tap_out[...] = whole
+
+    def send_taps(o, c):
+        remote(tap_out, tap_in.at[me], 11, {"ctx": far_first(o)}).start()
+        return c
+
+    lax.fori_loop(0, ctx - 1, send_taps, 0)
+    tap_in[pl.ds(me, 1)] = whole[None]
+    grad_skip[...] = swap_halves(whole)[1:2, : LANES // 2]
 
     edge_copy.wait()
     last = row_iota(16)
@@ -552,27 +606,6 @@
         done = tail[:, lanes] + (first_one * one + first_two * two) * e0 + (second_two * two) * e1
         grad_feats[rows - 16 :, lanes] = done.astype(BF16)
         return c
-
-    wait_all(part_in, 9, ctx - 1)
-    dp_out[...] = sum_slots(part_in, ctx)
-
-    def send_dp(o, c):
-        remote(dp_out, dp_in.at[my_dp], 10, {"dp": dp_peer(o)}).start()
-        return c
-
-    lax.fori_loop(1, dp, send_dp, 0)
-    dp_in[pl.ds(my_dp, 1)] = dp_out[...][None]
-    wait_all(dp_in, 10, dp - 1)
-    whole = sum_slots(dp_in, dp) * scale
-    tap_out[...] = whole
-
-    def send_taps(o, c):
-        remote(tap_out, tap_in.at[me], 11, {"ctx": peer_of(o)}).start()
-        return c
-
-    lax.fori_loop(1, ctx, send_taps, 0)
-    tap_in[pl.ds(me, 1)] = whole[None]
-    grad_skip[...] = swap_halves(whole)[1:2, : LANES // 2]
 
     lax.fori_loop(0, 3 * groups, finish, 0)
     wait_all(res_dp_in, 7, dp - 1)
@@ -606,6 +639,16 @@
         return c
 
     lax.fori_loop(0, groups, place_taps, 0, unroll=True)
+
+
+def write_out(*refs):
+    count = (len(refs) - 1) // 2
+    sems = refs[-1]
+    copies = [pltpu.make_async_copy(refs[k], refs[count + k], sems.at[k]) for k in range(count)]
+    for copy in copies:
+        copy.start()
+    for copy in copies:
+        copy.wait()
 
 
 def per_device(features, upstream, lengths, conv_taps, residues, log_rate, skip_gain):
@@ -636,7 +679,8 @@
         pltpu.VMEM(folded, F32),
         pltpu.VMEM(folded, F32),
         pltpu.VMEM((ctx, 1, LANES), F32),
-        pltpu.VMEM((SUBS, width), BF16),
+        pltpu.VMEM((2, width), F32),
+        pltpu.VMEM((2, width), F32),
         pltpu.VMEM(slab, BF16),
         pltpu.VMEM(slab, BF16),
         pltpu.VMEM(slab, BF16),
@@ -648,6 +692,7 @@
         wide,
         wide,
         wide,
+        pltpu.VMEM((SUBS, channels), F32),
         pltpu.VMEM((rows, channels), F32),
         pltpu.VMEM((rows, channels), F32),
         per_pole,
@@ -658,7 +703,7 @@
         per_pole,
         per_pole,
         pltpu.VMEM((groups, LANES), F32),
-        pltpu.VMEM((10, rows, LANES), F32),
+        pltpu.VMEM((12, rows, LANES), F32),
         pltpu.VMEM((2, width), F32),
         pltpu.VMEM((2, width), F32),
         pltpu.VMEM((16, width), F32),
@@ -676,22 +721,37 @@
         pltpu.SemaphoreType.DMA((12,)),
         pltpu.SemaphoreType.DMA((12,)),
     ]
-    grad_feats, grad_taps, grad_res, grad_skip = pl.pallas_call(
+    results = (
+        jax.ShapeDtypeStruct((rows, width), BF16),
+        jax.ShapeDtypeStruct((3, width), F32),
+        jax.ShapeDtypeStruct((poles, owned), F32),
+        jax.ShapeDtypeStruct((1, owned), F32),
+    )
+    held = pl.pallas_call(
         functools.partial(kernel, ctx, dp, scale),
-        out_shape=(
-            jax.ShapeDtypeStruct((rows, width), BF16),
-            jax.ShapeDtypeStruct((3, width), F32),
-            jax.ShapeDtypeStruct((poles, owned), F32),
-            jax.ShapeDtypeStruct((1, owned), F32),
-        ),
+        out_shape=results,
         in_specs=[smem] + [hbm] * 6,
         out_specs=(vmem,) * 4,
         scratch_shapes=scratch,
         compiler_params=pltpu.CompilerParams(
-            collective_id=0, has_side_effects=True, vmem_limit_bytes=56 * 1024 * 1024
+            collective_id=0, has_side_effects=True, vmem_limit_bytes=44 * 1024 * 1024
         ),
         name="conv_block",
-    )(lengths, features[0], upstream[0], conv_taps, residues, log_rate, skip_gain[None])
+    )(
+        *(
+            pltpu.with_memory_space_constraint(x, pltpu.HBM)
+            for x in (lengths, features[0], upstream[0], conv_taps, residues, log_rate, skip_gain[None])
+        )
+    )
+    grad_feats, grad_taps, grad_res, grad_skip = pl.pallas_call(
+        write_out,
+        out_shape=results,
+        in_specs=[vmem] * 4,
+        out_specs=(hbm,) * 4,
+        scratch_shapes=[pltpu.SemaphoreType.DMA((4,))],
+        compiler_params=pltpu.CompilerParams(vmem_limit_bytes=8 * 1024 * 1024),
+        name="write_out",
+    )(*held)
     return (grad_feats[None], grad_taps, grad_res, grad_skip[0])
 
 

time: 68.4 us -> 61 us (0.89)
  local copies, waits for them, and re-layouts: 4.49 us -> 0 us
  Pallas kernels: 63.1 us -> 60.2 us
    unnamed x10 -> x0, local copies, waits for them, and re-layouts: 4.49 us -> none
    pallas_call x1 -> x2, Pallas kernels: 63.1 us -> 60.2 us  [the longest x1 59 us: per_device(): pl.pallas_call(functools.partial(kernel, ctx, dp, scale), out_shape=resul...]
where the time goes in v3:
time: 61 us; the launch traced here: 60.8 us
  Pallas kernels  60.2 us (99%)
  between operations  0.64 us (1%)
    pallas_call x1, Pallas kernels, per_device(): pl.pallas_call(functools.partial(kernel, ctx, dp, scale), out_shape=resul...  59 us

profile of v3, /device:TPU:1, one launch (start us, length us, event | category | flops | bytes accessed | tf_op | source)
XLA Modules:
  0.0 60.8 jit_solution(6196683726254847312)
XLA Ops:
  0.6 59.0 %conv_block.1 = (bf16[128,6144]{1,0:T(8,128)(2,1)S(1)}, f32[3,6144]{1,0:T(4,128)S(1)}, f32[16,64]{1,0:T(8,128)S(1)}, f32[1,64]{1,0:T(1,128)S(1)}) custom-call(s32[1,8]{1,0:T(1,128)} %lengths.1, bf16[128,6144]{1,0:T(8,128)(2,1)} %bitcast.5, bf16[128,2048]{1,0:T(8,128)(2,1)} %bitcast.6, f32[3,6144]{1,0:T(4,128)} %taps_in.1, f32[16,64]{1,0:T(8,128)} %res_in.1, ...), custom_call_target="tpu_custom_call" | custom-call | tf_op jit(solution)/shard_map/conv_block/pallas_call | solution.py:730
  59.6 1.2 %write_out.1 = (bf16[128,6144]{1,0:T(8,128)(2,1)}, f32[3,6144]{1,0:T(4,128)}, f32[16,64]{1,0:T(8,128)}, f32[1,64]{1,0:T(1,128)}) custom-call(bf16[128,6144]{1,0:T(8,128)(2,1)S(1)} %get-tuple-element.12.refs_0_, f32[3,6144]{1,0:T(4,128)S(1)} %get-tuple-element.13.refs_1_, f32[16,64]{1,0:T(8,128)S(1)} %get-tuple-element.14.refs_2_, ...), custom_call_target="tpu_custom_call" | custom-call | tf_op jit(solution)/shard_map/write_out/pallas_call | solution.py:746

commit v4 on v3

--- a/solution.py
+++ b/solution.py
@@ -111,15 +111,15 @@
     masks,
     edge_out,
     edge_in,
-    tail,
+    posts,
     res_part_out,
     res_part_in,
     res_dp_out,
     res_dp_in,
     part_out,
     part_in,
-    dp_out,
-    dp_in,
+    column_out,
+    column_in,
     tap_out,
     tap_in,
     load_sem,
@@ -150,6 +150,18 @@
     def dp_peer(o):
         return lax.rem(my_dp + o, dp)
 
+    my_column, my_row = lax.rem(me, 8), lax.div(me, 8)
+    my_member = my_row * dp + my_dp
+
+    def member(j):
+        return {"ctx": lax.div(j, dp) * 8 + my_column, "dp": lax.rem(j, dp)}
+
+    def other_member(o):
+        return lax.rem(my_member + o, ctx)
+
+    def column_peer(o):
+        return {"ctx": my_row * 8 + lax.rem(my_column + o, 8)}
+
     loads = [
         pltpu.make_async_copy(src, dst, load_sem.at[k])
         for k, (src, dst) in enumerate(
@@ -165,19 +177,20 @@
     ]
     for load in loads:
         load.start()
+
     barrier = pltpu.get_barrier_semaphore()
 
     def greet(o, c):
-        pl.semaphore_signal(barrier, inc=1, device_id={"ctx": peer_of(o)}, device_id_type=MESH)
-        return c
-
-    lax.fori_loop(1, ctx, greet, 0)
-
-    def greet_dp(o, c):
-        pl.semaphore_signal(barrier, inc=1, device_id={"dp": dp_peer(o)}, device_id_type=MESH)
-        return c
-
-    lax.fori_loop(1, dp, greet_dp, 0)
+        pl.semaphore_signal(barrier, inc=1, device_id={"ctx": far_first(o)}, device_id_type=MESH)
+        return c
+
+    lax.fori_loop(0, ctx - 1, greet, 0)
+
+    def greet_member(o, c):
+        pl.semaphore_signal(barrier, inc=1, device_id=member(other_member(o)), device_id_type=MESH)
+        return c
+
+    lax.fori_loop(1, ctx, greet_member, 0)
 
     for load in loads[:3]:
         load.wait()
@@ -264,7 +277,7 @@
 
     lax.fori_loop(0, groups, enter, 0)
 
-    pl.semaphore_wait(barrier, ctx - 1 + dp - 1)
+    pl.semaphore_wait(barrier, 2 * (ctx - 1))
 
     def remote(src, dst, k, to):
         return pltpu.make_async_remote_copy(
@@ -518,9 +531,26 @@
         lax.fori_loop(0, rows // 4, add_carry, 0)
 
     first_keep, first_both, second_both = masks[0, 0:1, :], masks[1, 0:1, :], masks[1, 1:2, :]
-
-    def leave(s, c):
-        i = group_of(s)
+    my_x = lax.div(my_dp, 2)
+
+    def team_group(o):
+        k, j = lax.div(o, NEAR), lax.rem(o, NEAR)
+        x_off = 2 + (1 - 2 * lax.rem(k, 2)) * lax.div(k + 1, 2)
+        y_off = 2 + (1 - 2 * lax.rem(j, 2)) * lax.div(j + 1, 2)
+        return lax.rem(my_row + y_off, NEAR) * NEAR + lax.rem(my_x + x_off, NEAR)
+
+    def slot_of(i):
+        t = lax.rem(lax.div(i, NEAR) + NEAR - my_y + 2, NEAR)
+        z_off = lax.rem(lax.rem(i, NEAR) + NEAR - my_z, NEAR)
+        upper = lax.div(z_off, 2)
+        return ((1 - upper) * (3 - z_off) + upper * (z_off - 2)) * NEAR + t
+
+    def send_part(j):
+        remote(part_out.at[j], part_in.at[my_member], 9, member(j)).start()
+
+    def leave(o, c):
+        i = team_group(o)
+        s = slot_of(i)
         here = pl.ds(at(i, 0), LANES)
         out = output[strided(s, rows, half_rows), :].astype(BF16).astype(F32)
         mixed = adjoint[strided(s, rows, half_rows), :].astype(BF16).astype(F32)
@@ -529,6 +559,8 @@
         for third, post in enumerate((up * out, mixed * values[:, here], mixed * keys[:, here])):
             lanes = pl.ds(at(i, third), LANES)
             f = feats[:, lanes].astype(F32)
+            posts[:, lanes] = post
+            edge_out[:, lanes] = post[0:2]
             one = masks[6] * pltpu.roll(post, rows - 1, 0)
             two = masks[7] * pltpu.roll(post, rows - 2, 0)
             p0, p1 = post[0:1], post[1:2]
@@ -536,41 +568,50 @@
             sums.append(jnp.sum(post * f, axis=0, keepdims=True))
             sums.append(jnp.sum(one * f, axis=0, keepdims=True) + p0 * first_keep * h1)
             sums.append(jnp.sum(two * f, axis=0, keepdims=True) + p0 * first_both * h2 + p1 * second_both * h1)
-            edge_out[:, lanes] = post[0:2]
-            back = taps[0:1, lanes] * post + taps[1:2, lanes] * one + taps[2:3, lanes] * two
-            grad_feats[:, lanes] = back.astype(BF16)
-            tail[:, lanes] = back[rows - 16 :]
         top = jnp.concatenate(sums[:SUBS], axis=0)
         rest = jnp.concatenate([sums[SUBS], skip_sum[pl.ds(s, 1), :]] + sums[:6], axis=0)
         low, high = split_pair(top, rest)
         part_out[2 * i] = low
         part_out[2 * i + 1] = high
 
-        @pl.when(s > 0)
+        @pl.when(o > 0)
         def _():
-            j = group_of(s - 1)
-            send_slab(part_out, part_in, 9, 2 * j)
-            send_slab(part_out, part_in, 9, 2 * j + 1)
+            j = team_group(o - 1)
+            send_part(2 * j)
+            send_part(2 * j + 1)
 
         return c
 
     lax.fori_loop(0, groups, leave, 0)
+    mate = my_member + 1 - 2 * lax.rem(my_member, 2)
+    send_part(mate)
+    part_in[pl.ds(my_member, 1)] = part_out[pl.ds(my_member, 1)]
     edge_copy = remote(edge_out, edge_in, 8, {"ctx": peer_of(ctx - 1)})
     edge_copy.start()
-    send_slots(part_out, part_in, 9, groups - 1, groups)
 
     def sum_slots(buf, count):
         return lax.fori_loop(0, count, lambda k, acc: acc + buf[k], jnp.zeros((SUBS, LANES), F32), unroll=True)
 
     wait_all(part_in, 9, ctx - 1)
-    dp_out[...] = sum_slots(part_in, ctx)
-
-    def send_dp(o, c):
-        remote(dp_out, dp_in.at[my_dp], 10, {"dp": dp_peer(o)}).start()
-        return c
-
-    lax.fori_loop(1, dp, send_dp, 0)
-    dp_in[pl.ds(my_dp, 1)] = dp_out[...][None]
+    column_out[...] = sum_slots(part_in, ctx)
+
+    def send_column(o, c):
+        remote(column_out, column_in.at[my_column], 10, column_peer(o)).start()
+        return c
+
+    lax.fori_loop(1, 8, send_column, 0)
+    column_in[pl.ds(my_column, 1)] = column_out[...][None]
+    wait_all(column_in, 10, 7)
+    whole = sum_slots(column_in, 8) * scale
+    tap_out[...] = whole
+
+    def send_taps(o, c):
+        remote(tap_out, tap_in.at[my_member], 11, member(other_member(o))).start()
+        return c
+
+    lax.fori_loop(1, ctx, send_taps, 0)
+    tap_in[pl.ds(my_member, 1)] = whole[None]
+
     wait_all(res_part_in, 6, ctx - 1)
     res_dp_out[...] = sum_slots(res_part_in, ctx) + res_carried
 
@@ -580,31 +621,17 @@
 
     lax.fori_loop(1, dp, send_res, 0)
     res_dp_in[pl.ds(my_dp, 1)] = res_dp_out[...][None]
-    wait_all(dp_in, 10, dp - 1)
-    whole = sum_slots(dp_in, dp) * scale
-    tap_out[...] = whole
-
-    def send_taps(o, c):
-        remote(tap_out, tap_in.at[me], 11, {"ctx": far_first(o)}).start()
-        return c
-
-    lax.fori_loop(0, ctx - 1, send_taps, 0)
-    tap_in[pl.ds(me, 1)] = whole[None]
-    grad_skip[...] = swap_halves(whole)[1:2, : LANES // 2]
-
     edge_copy.wait()
-    last = row_iota(16)
-    one16, two16 = masks[2, rows - 16 :, :], masks[3, rows - 16 :, :]
-    first_one = jnp.where(last == 15, one16, 0.0)
-    first_two = jnp.where(last == 14, two16, 0.0)
-    second_two = jnp.where(last == 15, two16, 0.0)
 
     def finish(i, c):
         lanes = pl.ds(pl.multiple_of(i * LANES, LANES), LANES)
-        one, two = taps[1:2, lanes], taps[2:3, lanes]
-        e0, e1 = edge_in[0:1, lanes], edge_in[1:2, lanes]
-        done = tail[:, lanes] + (first_one * one + first_two * two) * e0 + (second_two * two) * e1
-        grad_feats[rows - 16 :, lanes] = done.astype(BF16)
+        post = posts[:, lanes]
+        after = jnp.where(head == 0, edge_in[0:1, lanes], edge_in[1:2, lanes])
+        ext = jnp.concatenate([post, after], axis=0)
+        one = masks[2] * pltpu.roll(ext, rows + SUBS - 1, 0)[:rows]
+        two = masks[3] * pltpu.roll(ext, rows + SUBS - 2, 0)[:rows]
+        back = taps[0:1, lanes] * post + taps[1:2, lanes] * one + taps[2:3, lanes] * two
+        grad_feats[:, lanes] = back.astype(BF16)
         return c
 
     lax.fori_loop(0, 3 * groups, finish, 0)
@@ -621,12 +648,13 @@
         (6, res_part_in, ctx),
         (7, res_dp_in, dp),
         (9, part_in, ctx),
-        (10, dp_in, dp),
+        (10, column_in, 8),
         (11, tap_in, ctx),
     ]:
         all_slots(buf, send_sem.at[k], slots - 1)
 
     wait_all(tap_in, 11, ctx - 1)
+    grad_skip[...] = swap_halves(tap_in[me])[1:2, : LANES // 2]
 
     def place_taps(i, c):
         low, high = tap_in[2 * i], tap_in[2 * i + 1]
@@ -706,7 +734,7 @@
         pltpu.VMEM((12, rows, LANES), F32),
         pltpu.VMEM((2, width), F32),
         pltpu.VMEM((2, width), F32),
-        pltpu.VMEM((16, width), F32),
+        pltpu.VMEM((rows, width), F32),
         pltpu.VMEM(folded, F32),
         pltpu.VMEM(folded, F32),
         pltpu.VMEM((SUBS, LANES), F32),
@@ -714,7 +742,7 @@
         pltpu.VMEM(folded, F32),
         pltpu.VMEM(folded, F32),
         pltpu.VMEM((SUBS, LANES), F32),
-        pltpu.VMEM((dp, SUBS, LANES), F32),
+        pltpu.VMEM((8, SUBS, LANES), F32),
         pltpu.VMEM((SUBS, LANES), F32),
         pltpu.VMEM(folded, F32),
         pltpu.SemaphoreType.DMA((6,)),

time: 61 us -> 60.2 us (0.987)
  Pallas kernels: 60.2 us -> 59.5 us
    pallas_call x1, Pallas kernels: 59 us -> 58.3 us  [per_device(): pl.pallas_call(functools.partial(kernel, ctx, dp, scale), out_shape=resul...]
where the time goes in v4:
time: 60.2 us; the launch traced here: 60.1 us
  Pallas kernels  59.5 us (99%)
  between operations  0.64 us (1%)
    pallas_call x1, Pallas kernels, per_device(): pl.pallas_call(functools.partial(kernel, ctx, dp, scale), out_shape=resul...  58.3 us

profile of v4, /device:TPU:1, one launch (start us, length us, event | category | flops | bytes accessed | tf_op | source)
XLA Modules:
  0.0 60.1 jit_solution(9890952207342767035)
XLA Ops:
  0.6 58.3 %conv_block.1 = (bf16[128,6144]{1,0:T(8,128)(2,1)S(1)}, f32[3,6144]{1,0:T(4,128)S(1)}, f32[16,64]{1,0:T(8,128)S(1)}, f32[1,64]{1,0:T(1,128)S(1)}) custom-call(s32[1,8]{1,0:T(1,128)} %lengths.1, bf16[128,6144]{1,0:T(8,128)(2,1)} %bitcast.5, bf16[128,2048]{1,0:T(8,128)(2,1)} %bitcast.6, f32[3,6144]{1,0:T(4,128)} %taps_in.1, f32[16,64]{1,0:T(8,128)} %res_in.1, ...), custom_call_target="tpu_custom_call" | custom-call | tf_op jit(solution)/shard_map/conv_block/pallas_call | solution.py:758
  58.9 1.2 %write_out.1 = (bf16[128,6144]{1,0:T(8,128)(2,1)}, f32[3,6144]{1,0:T(4,128)}, f32[16,64]{1,0:T(8,128)}, f32[1,64]{1,0:T(1,128)}) custom-call(bf16[128,6144]{1,0:T(8,128)(2,1)S(1)} %get-tuple-element.12.refs_0_, f32[3,6144]{1,0:T(4,128)S(1)} %get-tuple-element.13.refs_1_, f32[16,64]{1,0:T(8,128)S(1)} %get-tuple-element.14.refs_2_, ...), custom_call_target="tpu_custom_call" | custom-call | tf_op jit(solution)/shard_map/write_out/pallas_call | solution.py:774

commit v5 on v4

--- a/solution.py
+++ b/solution.py
@@ -548,41 +548,66 @@
     def send_part(j):
         remote(part_out.at[j], part_in.at[my_member], 9, member(j)).start()
 
-    def leave(o, c):
+    first_row, second_row = head == 0, head == 1
+    last_row, last_two = head == SUBS - 1, head >= SUBS - 2
+
+    def above(x, after, by):
+        edge = last_row if by == 1 else last_two
+        return jnp.where(edge, pltpu.roll(after, SUBS - by, 0), pltpu.roll(x, SUBS - by, 0))
+
+    def leave(o):
         i = team_group(o)
         s = slot_of(i)
         here = pl.ds(at(i, 0), LANES)
-        out = output[strided(s, rows, half_rows), :].astype(BF16).astype(F32)
-        mixed = adjoint[strided(s, rows, half_rows), :].astype(BF16).astype(F32)
-        up = upstream[:, here].astype(F32)
-        sums = []
-        for third, post in enumerate((up * out, mixed * values[:, here], mixed * keys[:, here])):
-            lanes = pl.ds(at(i, third), LANES)
-            f = feats[:, lanes].astype(F32)
-            posts[:, lanes] = post
-            edge_out[:, lanes] = post[0:2]
-            one = masks[6] * pltpu.roll(post, rows - 1, 0)
-            two = masks[7] * pltpu.roll(post, rows - 2, 0)
-            p0, p1 = post[0:1], post[1:2]
+        thirds = [pl.ds(at(i, third), LANES) for third in range(3)]
+        base = lax.div(s, SUBS) * half_rows + lax.rem(s, SUBS)
+        sums = [jnp.zeros((SUBS, LANES), F32)] * 9
+        after = [jnp.zeros((SUBS, LANES), F32)] * 3
+        for pair in reversed(range(rows // 16)):
+            rows16 = pl.ds(pair * 16, 16)
+            up16 = upstream[rows16, here].astype(F32)
+            f16 = [feats[rows16, lanes].astype(F32) for lanes in thirds]
+            for half in (1, 0):
+                r = pair * 16 + half * SUBS
+                tile = pl.ds(r, SUBS)
+                picked = pl.ds(base + r * SUBS, SUBS, stride=SUBS)
+                out = output[picked, :].astype(BF16).astype(F32)
+                mixed = adjoint[picked, :].astype(BF16).astype(F32)
+                part = slice(half * SUBS, (half + 1) * SUBS)
+                post = [up16[part] * out, mixed * values[tile, here], mixed * keys[tile, here]]
+                next_one, next_two = masks[6, tile, :], masks[7, tile, :]
+                for third in range(3):
+                    f = f16[third][part]
+                    posts[tile, thirds[third]] = post[third]
+                    sums[3 * third] = sums[3 * third] + post[third] * f
+                    sums[3 * third + 1] = sums[3 * third + 1] + next_one * above(post[third], after[third], 1) * f
+                    sums[3 * third + 2] = sums[3 * third + 2] + next_two * above(post[third], after[third], 2) * f
+                after = post
+        for third, lanes in enumerate(thirds):
+            edge_out[:, lanes] = after[third][0:2]
             h1, h2 = halo[1:2, lanes], halo[0:1, lanes]
-            sums.append(jnp.sum(post * f, axis=0, keepdims=True))
-            sums.append(jnp.sum(one * f, axis=0, keepdims=True) + p0 * first_keep * h1)
-            sums.append(jnp.sum(two * f, axis=0, keepdims=True) + p0 * first_both * h2 + p1 * second_both * h1)
+            sums[3 * third + 1] = sums[3 * third + 1] + jnp.where(first_row, after[third] * first_keep * h1, 0.0)
+            sums[3 * third + 2] = (
+                sums[3 * third + 2]
+                + jnp.where(first_row, after[third] * first_both * h2, 0.0)
+                + jnp.where(second_row, after[third] * second_both * h1, 0.0)
+            )
+        sums = [jnp.sum(x, axis=0, keepdims=True) for x in sums]
         top = jnp.concatenate(sums[:SUBS], axis=0)
         rest = jnp.concatenate([sums[SUBS], skip_sum[pl.ds(s, 1), :]] + sums[:6], axis=0)
         low, high = split_pair(top, rest)
         part_out[2 * i] = low
         part_out[2 * i + 1] = high
 
-        @pl.when(o > 0)
-        def _():
-            j = team_group(o - 1)
-            send_part(2 * j)
-            send_part(2 * j + 1)
-
-        return c
-
-    lax.fori_loop(0, groups, leave, 0)
+    def leave_and_send(o, c):
+        leave(o)
+        j = team_group(o - 1)
+        send_part(2 * j)
+        send_part(2 * j + 1)
+        return c
+
+    leave(0)
+    lax.fori_loop(1, groups, leave_and_send, 0)
     mate = my_member + 1 - 2 * lax.rem(my_member, 2)
     send_part(mate)
     part_in[pl.ds(my_member, 1)] = part_out[pl.ds(my_member, 1)]
@@ -592,6 +617,16 @@
     def sum_slots(buf, count):
         return lax.fori_loop(0, count, lambda k, acc: acc + buf[k], jnp.zeros((SUBS, LANES), F32), unroll=True)
 
+    wait_all(res_part_in, 6, ctx - 1)
+    res_dp_out[...] = sum_slots(res_part_in, ctx) + res_carried
+
+    def send_res(o, c):
+        remote(res_dp_out, res_dp_in.at[my_dp], 7, {"dp": dp_peer(o)}).start()
+        return c
+
+    lax.fori_loop(1, dp, send_res, 0)
+    res_dp_in[pl.ds(my_dp, 1)] = res_dp_out[...][None]
+
     wait_all(part_in, 9, ctx - 1)
     column_out[...] = sum_slots(part_in, ctx)
 
@@ -606,35 +641,39 @@
     tap_out[...] = whole
 
     def send_taps(o, c):
-        remote(tap_out, tap_in.at[my_member], 11, member(other_member(o))).start()
-        return c
-
-    lax.fori_loop(1, ctx, send_taps, 0)
+        i = team_group(o)
+        for j in (2 * i, 2 * i + 1):
+            remote(tap_out, tap_in.at[my_member], 11, member(j)).start()
+        return c
+
+    lax.fori_loop(0, groups - 1, send_taps, 0)
+    remote(tap_out, tap_in.at[my_member], 11, member(mate)).start()
     tap_in[pl.ds(my_member, 1)] = whole[None]
 
-    wait_all(res_part_in, 6, ctx - 1)
-    res_dp_out[...] = sum_slots(res_part_in, ctx) + res_carried
-
-    def send_res(o, c):
-        remote(res_dp_out, res_dp_in.at[my_dp], 7, {"dp": dp_peer(o)}).start()
-        return c
-
-    lax.fori_loop(1, dp, send_res, 0)
-    res_dp_in[pl.ds(my_dp, 1)] = res_dp_out[...][None]
     edge_copy.wait()
 
     def finish(i, c):
-        lanes = pl.ds(pl.multiple_of(i * LANES, LANES), LANES)
-        post = posts[:, lanes]
-        after = jnp.where(head == 0, edge_in[0:1, lanes], edge_in[1:2, lanes])
-        ext = jnp.concatenate([post, after], axis=0)
-        one = masks[2] * pltpu.roll(ext, rows + SUBS - 1, 0)[:rows]
-        two = masks[3] * pltpu.roll(ext, rows + SUBS - 2, 0)[:rows]
-        back = taps[0:1, lanes] * post + taps[1:2, lanes] * one + taps[2:3, lanes] * two
-        grad_feats[:, lanes] = back.astype(BF16)
-        return c
-
-    lax.fori_loop(0, 3 * groups, finish, 0)
+        thirds = [pl.ds(at(i, third), LANES) for third in range(3)]
+        after = [jnp.where(first_row, edge_in[0:1, lanes], edge_in[1:2, lanes]) for lanes in thirds]
+        for pair in reversed(range(rows // 16)):
+            done = [[], [], []]
+            for half in (1, 0):
+                tile = pl.ds(pair * 16 + half * SUBS, SUBS)
+                one, two = masks[2, tile, :], masks[3, tile, :]
+                for third, lanes in enumerate(thirds):
+                    post = posts[tile, lanes]
+                    back = (
+                        taps[0:1, lanes] * post
+                        + taps[1:2, lanes] * (one * above(post, after[third], 1))
+                        + taps[2:3, lanes] * (two * above(post, after[third], 2))
+                    )
+                    done[third].insert(0, back)
+                    after[third] = post
+            for third, lanes in enumerate(thirds):
+                grad_feats[pl.ds(pair * 16, 16), lanes] = jnp.concatenate(done[third], axis=0).astype(BF16)
+        return c
+
+    lax.fori_loop(0, groups, finish, 0)
     wait_all(res_dp_in, 7, dp - 1)
     res_whole = sum_slots(res_dp_in, dp) * scale
     grad_res[:SUBS, :] = res_whole[:, : LANES // 2]

time: 60.2 us -> 59.4 us (0.987)
  Pallas kernels: 59.5 us -> 58.7 us
    pallas_call x1, Pallas kernels: 58.3 us -> 57.5 us  [per_device(): pl.pallas_call(functools.partial(kernel, ctx, dp, scale), out_shape=resul...]
where the time goes in v5:
time: 59.4 us; the launch traced here: 59.3 us
  Pallas kernels  58.7 us (99%)
  between operations  0.64 us (1%)
    pallas_call x1, Pallas kernels, per_device(): pl.pallas_call(functools.partial(kernel, ctx, dp, scale), out_shape=resul...  57.5 us
    pallas_call x1, Pallas kernels, per_device(): pl.pallas_call(write_out, out_shape=results, in_specs=[vmem] * 4, out_spe...  1.2 us

profile of v5, /device:TPU:1, one launch (start us, length us, event | category | flops | bytes accessed | tf_op | source)
XLA Modules:
  0.0 59.3 jit_solution(13737628144330293734)
XLA Ops:
  0.6 57.5 %conv_block.1 = (bf16[128,6144]{1,0:T(8,128)(2,1)S(1)}, f32[3,6144]{1,0:T(4,128)S(1)}, f32[16,64]{1,0:T(8,128)S(1)}, f32[1,64]{1,0:T(1,128)S(1)}) custom-call(s32[1,8]{1,0:T(1,128)} %lengths.1, bf16[128,6144]{1,0:T(8,128)(2,1)} %bitcast.5, bf16[128,2048]{1,0:T(8,128)(2,1)} %bitcast.6, f32[3,6144]{1,0:T(4,128)} %taps_in.1, f32[16,64]{1,0:T(8,128)} %res_in.1, ...), custom_call_target="tpu_custom_call" | custom-call | tf_op jit(solution)/shard_map/conv_block/pallas_call | solution.py:797
  58.1 1.2 %write_out.1 = (bf16[128,6144]{1,0:T(8,128)(2,1)}, f32[3,6144]{1,0:T(4,128)}, f32[16,64]{1,0:T(8,128)}, f32[1,64]{1,0:T(1,128)}) custom-call(bf16[128,6144]{1,0:T(8,128)(2,1)S(1)} %get-tuple-element.12.refs_0_, f32[3,6144]{1,0:T(4,128)S(1)} %get-tuple-element.13.refs_1_, f32[16,64]{1,0:T(8,128)S(1)} %get-tuple-element.14.refs_2_, ...), custom_call_target="tpu_custom_call" | custom-call | tf_op jit(solution)/shard_map/write_out/pallas_call | solution.py:813

commit v6 on v5

--- a/solution.py
+++ b/solution.py
@@ -47,6 +47,10 @@
 
 def fold(x):
     return jnp.where(lane_low(SUBS), x[:SUBS], swap_halves(x[SUBS:]))
+
+
+FAR_Z = (4, 3, 5, 2, 6, 1, 7, 0)
+FAR = (2, 1, 3, 0)
 
 
 def free_of(bounds, low, high):
@@ -152,12 +156,22 @@
 
     my_column, my_row = lax.rem(me, 8), lax.div(me, 8)
     my_member = my_row * dp + my_dp
+    my_x, my_core = lax.div(my_dp, 2), lax.rem(my_dp, 2)
+    row_at = [lax.rem(my_row + k, 4) for k in range(4)]
+    column_at = [lax.rem(my_column + k, 8) for k in range(8)]
+    x_at = [lax.rem(my_x + k, 4) * 2 for k in range(4)]
+    core_at = [my_core, 1 - my_core]
+    far_ctx = [{"ctx": row_at[y] * 8 + column_at[z]} for z in FAR_Z for y in FAR if y or z]
+    far_team = [
+        {"ctx": row_at[y] * 8 + my_column, "dp": x_at[x] + core_at[c]}
+        for x in FAR
+        for y in FAR
+        for c in (1, 0)
+        if x or y or c
+    ]
 
     def member(j):
         return {"ctx": lax.div(j, dp) * 8 + my_column, "dp": lax.rem(j, dp)}
-
-    def other_member(o):
-        return lax.rem(my_member + o, ctx)
 
     def column_peer(o):
         return {"ctx": my_row * 8 + lax.rem(my_column + o, 8)}
@@ -180,17 +194,8 @@
 
     barrier = pltpu.get_barrier_semaphore()
 
-    def greet(o, c):
-        pl.semaphore_signal(barrier, inc=1, device_id={"ctx": far_first(o)}, device_id_type=MESH)
-        return c
-
-    lax.fori_loop(0, ctx - 1, greet, 0)
-
-    def greet_member(o, c):
-        pl.semaphore_signal(barrier, inc=1, device_id=member(other_member(o)), device_id_type=MESH)
-        return c
-
-    lax.fori_loop(1, ctx, greet_member, 0)
+    for to in far_ctx + far_team:
+        pl.semaphore_signal(barrier, inc=1, device_id=to, device_id_type=MESH)
 
     for load in loads[:3]:
         load.wait()
@@ -284,11 +289,8 @@
             src_ref=src, dst_ref=dst, send_sem=send_sem.at[k], recv_sem=recv_sem.at[k], device_id=to, device_id_type=MESH
         )
 
-    def send_rates(o, c):
-        remote(rate_out, rates.at[me], 1, {"ctx": far_first(o)}).start()
-        return c
-
-    lax.fori_loop(0, ctx - 1, send_rates, 0)
+    for to in far_ctx:
+        remote(rate_out, rates.at[me], 1, to).start()
     halo_copy = remote(halo_out, halo, 0, {"ctx": peer_of(1)})
     halo_copy.start()
 
@@ -412,15 +414,16 @@
     def raise_powers(h):
         pole_at = pl.ds(h * pole_rows, pole_rows)
         fac = decay[pole_at, :].reshape(poles, SUBS, LANES)
+        twice = fac * fac
 
         def step(k, e):
             for t in range(4):
-                e = e * fac
-                to = pl.multiple_of((h * rows + k * 4 + t) * pole_rows, pole_rows)
+                to = pl.multiple_of((h * (rows // 2) + k * 4 + t) * pole_rows, pole_rows)
                 powers[pl.ds(to, pole_rows), :] = e.reshape(pole_rows, LANES)
+                e = e * twice
             return e
 
-        lax.fori_loop(0, rows // 4, step, coeff[pole_at, :].reshape(poles, SUBS, LANES))
+        lax.fori_loop(0, rows // 8, step, coeff[pole_at, :].reshape(poles, SUBS, LANES) * fac)
 
     def half_sweep(h):
         both = pl.ds(h * SUBS, SUBS)
@@ -516,23 +519,23 @@
         s = state[pole_at, :].reshape(poles, SUBS, LANES)
         u = costate[pole_at, :].reshape(poles, SUBS, LANES)
 
+        fac = decay[pole_at, :].reshape(poles, SUBS, LANES)
+
         def add_carry(k, c):
             for j in range(4):
-                t = k * 4 + j
-                r = rows - 1 - t
-                e = powers[pl.ds(pl.multiple_of((h * rows + t) * pole_rows, pole_rows), pole_rows), :]
+                e = powers[pl.ds(pl.multiple_of((h * (rows // 2) + k * 4 + j) * pole_rows, pole_rows), pole_rows), :]
                 e = e.reshape(poles, SUBS, LANES)
-                at_t = pl.ds(pl.multiple_of(h * half_rows + t * SUBS, SUBS), SUBS)
-                at_r = pl.ds(pl.multiple_of(h * half_rows + r * SUBS, SUBS), SUBS)
-                output[at_t, :] = output[at_t, :] + masks[8, pl.ds(t, 1), :] * jnp.sum(e * s, axis=0)
-                adjoint[at_r, :] = adjoint[at_r, :] + masks[9, pl.ds(r, 1), :] * jnp.sum(e * u, axis=0)
+                for e, t in ((e, k * 8 + 2 * j), (e * fac, k * 8 + 2 * j + 1)):
+                    r = rows - 1 - t
+                    at_t = pl.ds(pl.multiple_of(h * half_rows + t * SUBS, SUBS), SUBS)
+                    at_r = pl.ds(pl.multiple_of(h * half_rows + r * SUBS, SUBS), SUBS)
+                    output[at_t, :] = output[at_t, :] + masks[8, pl.ds(t, 1), :] * jnp.sum(e * s, axis=0)
+                    adjoint[at_r, :] = adjoint[at_r, :] + masks[9, pl.ds(r, 1), :] * jnp.sum(e * u, axis=0)
             return c
 
-        lax.fori_loop(0, rows // 4, add_carry, 0)
+        lax.fori_loop(0, rows // 8, add_carry, 0)
 
     first_keep, first_both, second_both = masks[0, 0:1, :], masks[1, 0:1, :], masks[1, 1:2, :]
-    my_x = lax.div(my_dp, 2)
-
     def team_group(o):
         k, j = lax.div(o, NEAR), lax.rem(o, NEAR)
         x_off = 2 + (1 - 2 * lax.rem(k, 2)) * lax.div(k + 1, 2)
@@ -599,15 +602,22 @@
         part_out[2 * i] = low
         part_out[2 * i + 1] = high
 
-    def leave_and_send(o, c):
-        leave(o)
-        j = team_group(o - 1)
+    def send_group(o):
+        j = team_group(o)
         send_part(2 * j)
         send_part(2 * j + 1)
+
+    def send_and_leave(k, c):
+        send_group(2 * k - 2)
+        send_group(2 * k - 1)
+        leave(2 * k)
+        leave(2 * k + 1)
         return c
 
     leave(0)
-    lax.fori_loop(1, groups, leave_and_send, 0)
+    leave(1)
+    lax.fori_loop(1, groups // 2, send_and_leave, 0)
+    send_group(groups - 2)
     mate = my_member + 1 - 2 * lax.rem(my_member, 2)
     send_part(mate)
     part_in[pl.ds(my_member, 1)] = part_out[pl.ds(my_member, 1)]
@@ -640,14 +650,8 @@
     whole = sum_slots(column_in, 8) * scale
     tap_out[...] = whole
 
-    def send_taps(o, c):
-        i = team_group(o)
-        for j in (2 * i, 2 * i + 1):
-            remote(tap_out, tap_in.at[my_member], 11, member(j)).start()
-        return c
-
-    lax.fori_loop(0, groups - 1, send_taps, 0)
-    remote(tap_out, tap_in.at[my_member], 11, member(mate)).start()
+    for to in far_team:
+        remote(tap_out, tap_in.at[my_member], 11, to).start()
     tap_in[pl.ds(my_member, 1)] = whole[None]
 
     edge_copy.wait()
@@ -764,7 +768,7 @@
         pltpu.VMEM((rows, channels), F32),
         per_pole,
         per_pole,
-        pltpu.VMEM((rows * poles * groups, LANES), F32),
+        pltpu.VMEM((rows // 2 * poles * groups, LANES), F32),
         pltpu.VMEM((groups, LANES), F32),
         per_pole,
         per_pole,

time: 59.4 us -> 58 us (0.976)
  Pallas kernels: 58.7 us -> 57.2 us
    pallas_call x1, Pallas kernels: 57.5 us -> 56 us  [per_device(): pl.pallas_call(functools.partial(kernel, ctx, dp, scale), out_shape=resul...]
where the time goes in v6:
time: 58 us; the launch traced here: 57.8 us
  Pallas kernels  57.2 us (99%)
  between operations  0.64 us (1%)
    pallas_call x1, Pallas kernels, per_device(): pl.pallas_call(functools.partial(kernel, ctx, dp, scale), out_shape=resul...  56 us
    pallas_call x1, Pallas kernels, per_device(): pl.pallas_call(write_out, out_shape=results, in_specs=[vmem] * 4, out_spe...  1.2 us

profile of v6, /device:TPU:1, one launch (start us, length us, event | category | flops | bytes accessed | tf_op | source)
XLA Modules:
  0.0 57.8 jit_solution(101312526903891556)
XLA Ops:
  0.6 56.0 %conv_block.1 = (bf16[128,6144]{1,0:T(8,128)(2,1)S(1)}, f32[3,6144]{1,0:T(4,128)S(1)}, f32[16,64]{1,0:T(8,128)S(1)}, f32[1,64]{1,0:T(1,128)S(1)}) custom-call(s32[1,8]{1,0:T(1,128)} %lengths.1, bf16[128,6144]{1,0:T(8,128)(2,1)} %bitcast.5, bf16[128,2048]{1,0:T(8,128)(2,1)} %bitcast.6, f32[3,6144]{1,0:T(4,128)} %taps_in.1, f32[16,64]{1,0:T(8,128)} %res_in.1, ...), custom_call_target="tpu_custom_call" | custom-call | tf_op jit(solution)/shard_map/conv_block/pallas_call | solution.py:801
  56.6 1.2 %write_out.1 = (bf16[128,6144]{1,0:T(8,128)(2,1)}, f32[3,6144]{1,0:T(4,128)}, f32[16,64]{1,0:T(8,128)}, f32[1,64]{1,0:T(1,128)}) custom-call(bf16[128,6144]{1,0:T(8,128)(2,1)S(1)} %get-tuple-element.12.refs_0_, f32[3,6144]{1,0:T(4,128)S(1)} %get-tuple-element.13.refs_1_, f32[16,64]{1,0:T(8,128)S(1)} %get-tuple-element.14.refs_2_, ...), custom_call_target="tpu_custom_call" | custom-call | tf_op jit(solution)/shard_map/write_out/pallas_call | solution.py:817

commit v7 on v6

--- a/solution.py
+++ b/solution.py
@@ -220,27 +220,8 @@
     masks[2] = next_one
     masks[3] = next_two
 
-    masks[4] = free_of(bounds, pos + 1, flat + (start + rows - 1))
-    masks[5] = free_of(bounds, flat + (start + 1), pos)
-    masks[6] = jnp.where(row < rows - 1, next_one, 0.0)
-    masks[7] = jnp.where(row < rows - 2, next_two, 0.0)
-    masks[8] = free_of(bounds, flat + start, pos)
-    masks[9] = free_of(bounds, pos + 1, flat + (start + rows))
     masks[10] = jnp.where(row > 0, masks[0], 0.0)
     masks[11] = jnp.where(row > 1, masks[1], 0.0)
-
-    low16 = lane_low(poles)
-    my_rate = jnp.concatenate([own_rate[...], own_rate[...]], axis=1)
-    my_decay = jnp.exp(-jnp.exp(my_rate))
-    block_decay = jnp.exp(-jnp.exp(my_rate) * rows)
-
-    def join_masks(k, c):
-        low = jnp.where(low16, k * rows, (ctx - 1 - k) * rows + 1)
-        joins[k] = free_of(bounds, low, low + (rows - 1)) * block_decay
-        keeps[k] = free_of(bounds, low, low) * my_decay
-        return c
-
-    lax.fori_loop(0, ctx, join_masks, 0)
 
     my_y, my_z = lax.div(me, 2 * NEAR), lax.rem(lax.div(me, 2), NEAR)
 
@@ -303,6 +284,26 @@
     rates[pl.ds(me, 1)] = rate_out[...][None]
     residues[pl.ds(me, 1)] = res_out[...][None]
     skips[pl.ds(me, 1)] = skip_out[...][None]
+
+    masks[4] = free_of(bounds, pos + 1, flat + (start + rows - 1))
+    masks[5] = free_of(bounds, flat + (start + 1), pos)
+    masks[6] = jnp.where(row < rows - 1, next_one, 0.0)
+    masks[7] = jnp.where(row < rows - 2, next_two, 0.0)
+    masks[8] = free_of(bounds, flat + start, pos)
+    masks[9] = free_of(bounds, pos + 1, flat + (start + rows))
+
+    low16 = lane_low(poles)
+    my_rate = jnp.concatenate([own_rate[...], own_rate[...]], axis=1)
+    my_decay = jnp.exp(-jnp.exp(my_rate))
+    block_decay = jnp.exp(-jnp.exp(my_rate) * rows)
+
+    def join_masks(k, c):
+        low = jnp.where(low16, k * rows, (ctx - 1 - k) * rows + 1)
+        joins[k] = free_of(bounds, low, low + (rows - 1)) * block_decay
+        keeps[k] = free_of(bounds, low, low) * my_decay
+        return c
+
+    lax.fori_loop(0, ctx, join_masks, 0)
 
     halo_copy.wait()
     head = row_iota(SUBS)
@@ -344,23 +345,19 @@
 
     lax.fori_loop(0, groups, spread_rates, 0, unroll=True)
 
-    def send_slab(out, into, k, to):
-        @pl.when(to != me)
-        def _():
-            remote(out.at[to], into.at[me], k, {"ctx": to}).start()
-
-        @pl.when(to == me)
-        def _():
-            into[pl.ds(me, 1)] = out[pl.ds(me, 1)]
+    own_slot = 14
 
     def send_slots(out, into, k, low, high):
-        def send(s, c):
-            i = group_of(s)
-            send_slab(out, into, k, 2 * i)
-            send_slab(out, into, k, 2 * i + 1)
-            return c
-
-        lax.fori_loop(low, high, send, 0)
+        for s in range(low, high):
+            b, t = divmod(s, NEAR)
+            i = row_at[(t + 2) % NEAR] * NEAR + lax.rem(my_z + (2, 3, 1, 0)[b], NEAR)
+            if s == own_slot:
+                mate = me + 1 - 2 * lax.rem(me, 2)
+                remote(out.at[mate], into.at[me], k, {"ctx": mate}).start()
+                into[pl.ds(me, 1)] = out[pl.ds(me, 1)]
+            else:
+                for j in (2 * i, 2 * i + 1):
+                    remote(out.at[j], into.at[me], k, {"ctx": j}).start()
 
     for h in range(halves):
         pole_at = pl.ds(h * pole_rows, pole_rows)
@@ -715,7 +712,11 @@
 def write_out(*refs):
     count = (len(refs) - 1) // 2
     sems = refs[-1]
-    copies = [pltpu.make_async_copy(refs[k], refs[count + k], sems.at[k]) for k in range(count)]
+    copies = [pltpu.make_async_copy(refs[k], refs[count + k], sems.at[k]) for k in range(1, count)]
+    quarter = refs[0].shape[0] // 4
+    for k in range(4):
+        part = pl.ds(k * quarter, quarter)
+        copies.append(pltpu.make_async_copy(refs[0].at[part], refs[count].at[part], sems.at[count + k]))
     for copy in copies:
         copy.start()
     for copy in copies:
@@ -819,7 +820,7 @@
         out_shape=results,
         in_specs=[vmem] * 4,
         out_specs=(hbm,) * 4,
-        scratch_shapes=[pltpu.SemaphoreType.DMA((4,))],
+        scratch_shapes=[pltpu.SemaphoreType.DMA((8,))],
         compiler_params=pltpu.CompilerParams(vmem_limit_bytes=8 * 1024 * 1024),
         name="write_out",
     )(*held)

time: 58 us -> 56.6 us (0.976)
  Pallas kernels: 57.2 us -> 55.8 us
    pallas_call x1, Pallas kernels: 56 us -> 54.5 us  [per_device(): pl.pallas_call(functools.partial(kernel, ctx, dp, scale), out_shape=resul...]
where the time goes in v7:
time: 56.6 us; the launch traced here: 56.4 us
  Pallas kernels  55.8 us (99%)
  between operations  0.64 us (1%)
    pallas_call x1, Pallas kernels, per_device(): pl.pallas_call(functools.partial(kernel, ctx, dp, scale), out_shape=resul...  54.5 us
    pallas_call x1, Pallas kernels, per_device(): pl.pallas_call(write_out, out_shape=results, in_specs=[vmem] * 4, out_spe...  1.25 us

profile of v7, /device:TPU:1, one launch (start us, length us, event | category | flops | bytes accessed | tf_op | source)
XLA Modules:
  0.0 56.4 jit_solution(18243810678842531270)
XLA Ops:
  0.6 54.5 %conv_block.1 = (bf16[128,6144]{1,0:T(8,128)(2,1)S(1)}, f32[3,6144]{1,0:T(4,128)S(1)}, f32[16,64]{1,0:T(8,128)S(1)}, f32[1,64]{1,0:T(1,128)S(1)}) custom-call(s32[1,8]{1,0:T(1,128)} %lengths.1, bf16[128,6144]{1,0:T(8,128)(2,1)} %bitcast.5, bf16[128,2048]{1,0:T(8,128)(2,1)} %bitcast.6, f32[3,6144]{1,0:T(4,128)} %taps_in.1, f32[16,64]{1,0:T(8,128)} %res_in.1, ...), custom_call_target="tpu_custom_call" | custom-call | tf_op jit(solution)/shard_map/conv_block/pallas_call | solution.py:802
  55.2 1.2 %write_out.1 = (bf16[128,6144]{1,0:T(8,128)(2,1)}, f32[3,6144]{1,0:T(4,128)}, f32[16,64]{1,0:T(8,128)}, f32[1,64]{1,0:T(1,128)}) custom-call(bf16[128,6144]{1,0:T(8,128)(2,1)S(1)} %get-tuple-element.12.refs_0_, f32[3,6144]{1,0:T(4,128)S(1)} %get-tuple-element.13.refs_1_, f32[16,64]{1,0:T(8,128)S(1)} %get-tuple-element.14.refs_2_, ...), custom_call_target="tpu_custom_call" | custom-call | tf_op jit(solution)/shard_map/write_out/pallas_call | solution.py:818

commit v8 on v7

--- a/solution.py
+++ b/solution.py
@@ -51,6 +51,8 @@
 
 FAR_Z = (4, 3, 5, 2, 6, 1, 7, 0)
 FAR = (2, 1, 3, 0)
+TEAM_X = sum(v << (2 * k) for k, v in enumerate((2, 2, 2, 1, 3, 2, 0, 1, 1, 3, 3, 1, 3, 0, 0, 0)))
+TEAM_Y = sum(v << (2 * k) for k, v in enumerate((2, 1, 3, 2, 2, 0, 2, 1, 3, 1, 3, 0, 0, 1, 3, 0)))
 
 
 def free_of(bounds, low, high):
@@ -203,6 +205,31 @@
     res_out[...] = jnp.concatenate([own_res[:SUBS, :], own_res[SUBS:, :]], axis=1)
     skip_out[...] = jnp.concatenate([own_skip[...], own_skip[...]], axis=1)
 
+    pl.semaphore_wait(barrier, 2 * (ctx - 1))
+
+    def remote(src, dst, k, to):
+        return pltpu.make_async_remote_copy(
+            src_ref=src, dst_ref=dst, send_sem=send_sem.at[k], recv_sem=recv_sem.at[k], device_id=to, device_id_type=MESH
+        )
+
+    for to in far_ctx:
+        remote(rate_out, rates.at[me], 1, to).start()
+    for load in loads[3:]:
+        load.wait()
+    halo_out[...] = feats[rows - 16 :, :].astype(F32)[14:]
+    halo_copy = remote(halo_out, halo, 0, {"ctx": peer_of(1)})
+
+    def send_others(o, c):
+        remote(res_out, residues.at[me], 2, {"ctx": far_first(o)}).start()
+        remote(skip_out, skips.at[me], 3, {"ctx": far_first(o)}).start()
+        return c
+
+    lax.fori_loop(0, ctx - 1, send_others, 0)
+    halo_copy.start()
+    rates[pl.ds(me, 1)] = rate_out[...][None]
+    residues[pl.ds(me, 1)] = res_out[...][None]
+    skips[pl.ds(me, 1)] = skip_out[...][None]
+
     bounds = [0]
     total = 0
     for j in range(lengths.shape[1] - 1):
@@ -238,15 +265,11 @@
     def strided(s, count, stride_rows):
         return pl.ds(lax.div(s, SUBS) * stride_rows + lax.rem(s, SUBS), count, stride=SUBS)
 
-    for load in loads[3:]:
-        load.wait()
-
     def featured(off):
         lanes = pl.ds(off, LANES)
         f = feats[:, lanes].astype(F32)
         one = masks[10] * pltpu.roll(f, 1, 0)
         two = masks[11] * pltpu.roll(f, 2, 0)
-        halo_out[:, lanes] = f[rows - 2 :]
         return taps[0:1, lanes] * f + taps[1:2, lanes] * one + taps[2:3, lanes] * two
 
     def enter(s, c):
@@ -262,28 +285,6 @@
         return c
 
     lax.fori_loop(0, groups, enter, 0)
-
-    pl.semaphore_wait(barrier, 2 * (ctx - 1))
-
-    def remote(src, dst, k, to):
-        return pltpu.make_async_remote_copy(
-            src_ref=src, dst_ref=dst, send_sem=send_sem.at[k], recv_sem=recv_sem.at[k], device_id=to, device_id_type=MESH
-        )
-
-    for to in far_ctx:
-        remote(rate_out, rates.at[me], 1, to).start()
-    halo_copy = remote(halo_out, halo, 0, {"ctx": peer_of(1)})
-    halo_copy.start()
-
-    def send_others(o, c):
-        remote(res_out, residues.at[me], 2, {"ctx": far_first(o)}).start()
-        remote(skip_out, skips.at[me], 3, {"ctx": far_first(o)}).start()
-        return c
-
-    lax.fori_loop(0, ctx - 1, send_others, 0)
-    rates[pl.ds(me, 1)] = rate_out[...][None]
-    residues[pl.ds(me, 1)] = res_out[...][None]
-    skips[pl.ds(me, 1)] = skip_out[...][None]
 
     masks[4] = free_of(bounds, pos + 1, flat + (start + rows - 1))
     masks[5] = free_of(bounds, flat + (start + 1), pos)
@@ -534,9 +535,9 @@
 
     first_keep, first_both, second_both = masks[0, 0:1, :], masks[1, 0:1, :], masks[1, 1:2, :]
     def team_group(o):
-        k, j = lax.div(o, NEAR), lax.rem(o, NEAR)
-        x_off = 2 + (1 - 2 * lax.rem(k, 2)) * lax.div(k + 1, 2)
-        y_off = 2 + (1 - 2 * lax.rem(j, 2)) * lax.div(j + 1, 2)
+        shift = jnp.int32(2) * o
+        x_off = (jnp.int32(TEAM_X) >> shift) & 3
+        y_off = (jnp.int32(TEAM_Y) >> shift) & 3
         return lax.rem(my_row + y_off, NEAR) * NEAR + lax.rem(my_x + x_off, NEAR)
 
     def slot_of(i):

time: 56.6 us -> 58.1 us (1.027)
  Pallas kernels: 55.8 us -> 57.4 us
    pallas_call x1, Pallas kernels: 54.5 us -> 56.1 us  [per_device(): pl.pallas_call(functools.partial(kernel, ctx, dp, scale), out_shape=resul...]
where the time goes in v8:
time: 58.1 us; the launch traced here: 58 us
  Pallas kernels  57.4 us (99%)
  between operations  0.64 us (1%)
    pallas_call x1, Pallas kernels, per_device(): pl.pallas_call(functools.partial(kernel, ctx, dp, scale), out_shape=resul...  56.1 us
    pallas_call x1, Pallas kernels, per_device(): pl.pallas_call(write_out, out_shape=results, in_specs=[vmem] * 4, out_spe...  1.25 us

profile of v8, /device:TPU:1, one launch (start us, length us, event | category | flops | bytes accessed | tf_op | source)
XLA Modules:
  0.0 58.0 jit_solution(16892931629153545957)
XLA Ops:
  0.6 56.1 %conv_block.1 = (bf16[128,6144]{1,0:T(8,128)(2,1)S(1)}, f32[3,6144]{1,0:T(4,128)S(1)}, f32[16,64]{1,0:T(8,128)S(1)}, f32[1,64]{1,0:T(1,128)S(1)}) custom-call(s32[1,8]{1,0:T(1,128)} %lengths.1, bf16[128,6144]{1,0:T(8,128)(2,1)} %bitcast.5, bf16[128,2048]{1,0:T(8,128)(2,1)} %bitcast.6, f32[3,6144]{1,0:T(4,128)} %taps_in.1, f32[16,64]{1,0:T(8,128)} %res_in.1, ...), custom_call_target="tpu_custom_call" | custom-call | tf_op jit(solution)/shard_map/conv_block/pallas_call | solution.py:803
  56.8 1.2 %write_out.1 = (bf16[128,6144]{1,0:T(8,128)(2,1)}, f32[3,6144]{1,0:T(4,128)}, f32[16,64]{1,0:T(8,128)}, f32[1,64]{1,0:T(1,128)}) custom-call(bf16[128,6144]{1,0:T(8,128)(2,1)S(1)} %get-tuple-element.12.refs_0_, f32[3,6144]{1,0:T(4,128)S(1)} %get-tuple-element.13.refs_1_, f32[16,64]{1,0:T(8,128)S(1)} %get-tuple-element.14.refs_2_, ...), custom_call_target="tpu_custom_call" | custom-call | tf_op jit(solution)/shard_map/write_out/pallas_call | solution.py:819

commit v9 on v7

--- a/solution.py
+++ b/solution.py
@@ -51,6 +51,8 @@
 
 FAR_Z = (4, 3, 5, 2, 6, 1, 7, 0)
 FAR = (2, 1, 3, 0)
+TEAM_X = sum(v << (2 * k) for k, v in enumerate((2, 2, 2, 1, 3, 2, 0, 1, 1, 3, 3, 1, 3, 0, 0, 0)))
+TEAM_Y = sum(v << (2 * k) for k, v in enumerate((2, 1, 3, 2, 2, 0, 2, 1, 3, 1, 3, 0, 0, 1, 3, 0)))
 
 
 def free_of(bounds, low, high):
@@ -534,9 +536,9 @@
 
     first_keep, first_both, second_both = masks[0, 0:1, :], masks[1, 0:1, :], masks[1, 1:2, :]
     def team_group(o):
-        k, j = lax.div(o, NEAR), lax.rem(o, NEAR)
-        x_off = 2 + (1 - 2 * lax.rem(k, 2)) * lax.div(k + 1, 2)
-        y_off = 2 + (1 - 2 * lax.rem(j, 2)) * lax.div(j + 1, 2)
+        shift = jnp.int32(2) * o
+        x_off = (jnp.int32(TEAM_X) >> shift) & 3
+        y_off = (jnp.int32(TEAM_Y) >> shift) & 3
         return lax.rem(my_row + y_off, NEAR) * NEAR + lax.rem(my_x + x_off, NEAR)
 
     def slot_of(i):

time: 56.6 us -> 56.3 us (level)
  no operation moved by 1% of the time
where the time goes in v9:
time: 56.3 us; the launch traced here: 56.1 us
  Pallas kernels  55.5 us (99%)
  between operations  0.64 us (1%)
    pallas_call x1, Pallas kernels, per_device(): pl.pallas_call(functools.partial(kernel, ctx, dp, scale), out_shape=resul...  54.2 us
    pallas_call x1, Pallas kernels, per_device(): pl.pallas_call(write_out, out_shape=results, in_specs=[vmem] * 4, out_spe...  1.25 us

profile of v9, /device:TPU:1, one launch (start us, length us, event | category | flops | bytes accessed | tf_op | source)
XLA Modules:
  0.0 56.1 jit_solution(5405045011323231787)
XLA Ops:
  0.6 54.2 %conv_block.1 = (bf16[128,6144]{1,0:T(8,128)(2,1)S(1)}, f32[3,6144]{1,0:T(4,128)S(1)}, f32[16,64]{1,0:T(8,128)S(1)}, f32[1,64]{1,0:T(1,128)S(1)}) custom-call(s32[1,8]{1,0:T(1,128)} %lengths.1, bf16[128,6144]{1,0:T(8,128)(2,1)} %bitcast.5, bf16[128,2048]{1,0:T(8,128)(2,1)} %bitcast.6, f32[3,6144]{1,0:T(4,128)} %taps_in.1, f32[16,64]{1,0:T(8,128)} %res_in.1, ...), custom_call_target="tpu_custom_call" | custom-call | tf_op jit(solution)/shard_map/conv_block/pallas_call | solution.py:804
  54.9 1.2 %write_out.1 = (bf16[128,6144]{1,0:T(8,128)(2,1)}, f32[3,6144]{1,0:T(4,128)}, f32[16,64]{1,0:T(8,128)}, f32[1,64]{1,0:T(1,128)}) custom-call(bf16[128,6144]{1,0:T(8,128)(2,1)S(1)} %get-tuple-element.12.refs_0_, f32[3,6144]{1,0:T(4,128)S(1)} %get-tuple-element.13.refs_1_, f32[16,64]{1,0:T(8,128)S(1)} %get-tuple-element.14.refs_2_, ...), custom_call_target="tpu_custom_call" | custom-call | tf_op jit(solution)/shard_map/write_out/pallas_call | solution.py:820
